TPU v7x, 128 devices: a whole 4x4x4 slice. The times are simulated.
128 devices in a mesh: fiber: 2 (over z_lo), blk: 64 (over z_hi, x, y, core).
Axes of the slice: x: 4, y: 4, z: 4 (z_hi: 2, z_lo: 2; z = z_hi * 2 + z_lo), core: 2. Of those that a mesh axis runs over, the one named last changes fastest.
Arguments:
- users: bfloat16 [131072, 256], P('blk', 'fiber'), may hold values from -1.5 to 1.5
- items: bfloat16 [16384, 256], P('blk'), may hold values from -1.5 to 1.5
- tile_users: int32 [64, 2, 512], P('blk', 'fiber'), may hold values from 0 to 15
- tile_items: int32 [64, 2, 512], P('blk', 'fiber'), may hold values from 0 to 127, as said below
- confidence: bfloat16 [64, 2, 512, 128, 128], P('blk', 'fiber'), may hold values from 0.19921875 to 5
Outputs:
- user_grad: bfloat16 [131072, 256], P('blk', 'fiber')
Inputs may be any that keep to these rules, and one draw needn't show every extreme that they name: `tile_items`: each device's list is sorted by item block, then user block, and holds distinct pairs; the two lists of the same index of blk share no pair. A device has at most 8 tiles in any item block, and exactly 8 in at least one.
All inputs are finite; a program needn't handle non-finite values.
Results may differ from a plain program's by a relative error of at most 0.0034.
Values may be sent and summed in bfloat16 or wider, within the bound.
A program may use at most 128 MiB of HBM per device.

v0:
```python
import math

import jax
import jax.numpy as jnp
from jax import lax
from jax.sharding import PartitionSpec as P


def shards(users, items, tile_users, tile_items, confidence):
    panel_rows = lax.all_gather(users, "fiber", axis=1, tiled=True)
    tile_size = confidence.shape[-1]
    rank_width = panel_rows.shape[1]
    user_count = panel_rows.shape[0] // tile_size
    panel_blocks = panel_rows.reshape(user_count, tile_size, rank_width)
    user_list = tile_users.reshape(-1)
    item_list = tile_items.reshape(-1)
    conf_tiles = confidence.reshape(-1, tile_size, tile_size)
    tile_count = user_list.shape[0]
    item_count = items.shape[0] // tile_size * lax.axis_size("blk")
    block_ids = jnp.arange(user_count, dtype=jnp.int32)

    def accumulate(totals, user_ids, conf_part, item_rows, live_mask):
        user_rows = panel_blocks[user_ids]
        scores = jnp.einsum(
            "tar,tbr->tab", user_rows, item_rows, preferred_element_type=jnp.float32
        )
        weight = (conf_part.astype(jnp.float32) * (1.0 - scores) * live_mask[:, None, None]).astype(
            jnp.bfloat16
        )
        products = jnp.einsum("tab,tbr->tar", weight, item_rows, preferred_element_type=jnp.float32)
        return totals.at[user_ids].add(products)

    empty = jnp.zeros((user_count, tile_size, rank_width), jnp.float32)
    gathered = lax.all_gather(items, "blk", axis=0, tiled=True).reshape(
        item_count, tile_size, rank_width
    )
    group = math.gcd(tile_count, 128)
    every_live = jnp.ones((group,), jnp.float32)

    def one_group(index, running):
        first = (index * group).astype(jnp.int32)
        user_ids = lax.dynamic_slice_in_dim(user_list, first, group, 0)
        item_ids = lax.dynamic_slice_in_dim(item_list, first, group, 0)
        conf_part = lax.dynamic_slice_in_dim(conf_tiles, first, group, 0)
        return accumulate(running, user_ids, conf_part, gathered[item_ids], every_live)

    totals = lax.fori_loop(0, tile_count // group, one_group, empty)
    row_sums = jnp.sum(conf_tiles, axis=-1, dtype=jnp.float32)
    owners = (user_list[:, None] == block_ids[None, :]).astype(jnp.float32)
    row_local = jnp.einsum("tk,ta->ka", owners, row_sums, precision=lax.Precision.HIGHEST).reshape(
        -1
    )
    fiber_count = lax.axis_size("fiber")
    widened = jnp.broadcast_to(row_local[:, None], (row_local.shape[0], fiber_count))
    shares, row_total = (
        lax.psum_scatter(totals.reshape(-1, rank_width), "fiber", scatter_dimension=1, tiled=True),
        lax.psum_scatter(widened, "fiber", scatter_dimension=1, tiled=True),
    )
    return (shares * lax.rsqrt(1.0 + row_total)).astype(jnp.bfloat16)


def solution(mesh):
    in_specs = (
        P("blk", "fiber"),
        P("blk", None),
        P("blk", "fiber", None),
        P("blk", "fiber", None),
        P("blk", "fiber", None, None, None),
    )
    out_specs = P("blk", "fiber")
    return jax.shard_map(shards, mesh=mesh, in_specs=in_specs, out_specs=out_specs, check_vma=False)
```

profile of v0, /device:TPU:1, one launch (start us, length us, event | category | flops | bytes accessed | tf_op | source)
XLA Modules:
  0.0 407.1 jit_solution(5463470530003183138)
XLA Ops:
  8.1 28.1 %all-gather.3.cloned.1.call-done = bf16[2048,256]{1,0:T(8,128)(2,1)} async-done(((bf16[2048,128]{1,0:T(8,128)(2,1)}), bf16[2048,256]{1,0:T(8,128)(2,1)}) %all-gather.3.cloned.1.call-update) | async-done | bytes 1048592 | tf_op jit(solution)/shard_map/all_gather | solution.py:10
  36.1 88.2 %all-gather.5.cloned.1.call-done = bf16[16384,256]{1,0:T(8,128)(2,1)} async-done(((bf16[256,256]{1,0:T(8,128)(2,1)}), bf16[16384,256]{1,0:T(8,128)(2,1)}) %all-gather.5.cloned.1.call-update) | async-done | bytes 8388624 | tf_op jit(solution)/shard_map/all_gather | solution.py:34
  124.6 241.1 %while.13 = (s32[]{:T(128)}, f32[16,128,256]{2,1,0:T(8,128)S(1)}, s32[512]{0:T(512)}, bf16[512,128,128]{2,1,0:T(8,128)(2,1)}, bf16[16,128,256]{2,1,0:T(8,128)(2,...) while((s32[]{:T(128)}, f32[16,128,256]{2,1,0:T(8,128)S(1)}, ...), condition=%wide.region_2.0_spmd, body=%wide.region_0.0_spmd.sunk | while | flops 2160069376 | bytes 130036384 | solution.py:47
  125.4 7.8 %gather_fusion.1 = bf16[128,128,256]{2,1,0:T(8,128)(2,1)} fusion(bf16[16,128,256]{2,1,0:T(8,128)(2,1)} %get-tuple-element.219, s32[1024]{0:T(1024)S(1)} %pad_clamp_fusion.5), kind=kCustom, calls=%fused_computation.clone.1 | custom fusion | bytes 16777728 | tf_op jit(solution)/shard_map/while/body/eval_jaxpr/gather | solution.py:23
  133.2 9.9 %gather_fusion = bf16[128,128,256]{2,1,0:T(8,128)(2,1)} fusion(bf16[128,128,256]{2,1,0:T(8,128)(2,1)} %get-tuple-element.221, s32[1024]{0:T(1024)S(1)} %pad_clamp_fusion.4), kind=kCustom, calls=%fused_computation.1.clone.1 | custom fusion | bytes 16777728 | tf_op jit(solution)/shard_map/while/body/eval_jaxpr/gather | solution.py:45
  143.1 17.4 %fusion.20 = f32[128,128,256]{2,1,0:T(8,128)} fusion(bf16[128,128,256]{2,1,0:T(8,128)(2,1)} %gather_fusion, bf16[512,128,128]{2,1,0:T(8,128)(2,1)} %get-tuple-element.218, s32[]{:T(128)S(6)} %select_n.29, bf16[128,128,256]{2,1,0:T(8,128)(2,1)} %gather_fusion.1), kind=kOutput, calls=%fused_computation.4.clone.1 | convolution fusion | flops 2155872256 | bytes 46137348 | tf_op jit(solution)/shard_map/while/body/eval_jaxpr/tab,tbr->tar/dot_general | solution.py:30
  160.5 24.3 %scatter_fusion = f32[16,128,256]{2,1,0:T(8,128)S(1)} fusion(f32[16,128,256]{2,1,0:T(8,128)S(1)} %get-tuple-element.205, s32[128]{0:T(128)S(1)} %get-tuple-element.191, f32[128,128,256]{2,1,0:T(8,128)} %fusion.20), kind=kCustom, calls=%fused_computation.2.clone.1 | custom fusion | flops 4194304 | bytes 50332160 | tf_op jit(solution)/shard_map/while/body/eval_jaxpr/scatter-add | solution.py:31
  185.7 7.7 %gather_fusion.1 = bf16[128,128,256]{2,1,0:T(8,128)(2,1)} fusion(bf16[16,128,256]{2,1,0:T(8,128)(2,1)} %get-tuple-element.219, s32[1024]{0:T(1024)S(1)} %pad_clamp_fusion.5), kind=kCustom, calls=%fused_computation.clone.1 | custom fusion | bytes 16777728 | tf_op jit(solution)/shard_map/while/body/eval_jaxpr/gather | solution.py:23
  193.5 9.9 %gather_fusion = bf16[128,128,256]{2,1,0:T(8,128)(2,1)} fusion(bf16[128,128,256]{2,1,0:T(8,128)(2,1)} %get-tuple-element.221, s32[1024]{0:T(1024)S(1)} %pad_clamp_fusion.4), kind=kCustom, calls=%fused_computation.1.clone.1 | custom fusion | bytes 16777728 | tf_op jit(solution)/shard_map/while/body/eval_jaxpr/gather | solution.py:45
  203.4 17.3 %fusion.20 = f32[128,128,256]{2,1,0:T(8,128)} fusion(bf16[128,128,256]{2,1,0:T(8,128)(2,1)} %gather_fusion, bf16[512,128,128]{2,1,0:T(8,128)(2,1)} %get-tuple-element.218, s32[]{:T(128)S(6)} %select_n.29, bf16[128,128,256]{2,1,0:T(8,128)(2,1)} %gather_fusion.1), kind=kOutput, calls=%fused_computation.4.clone.1 | convolution fusion | flops 2155872256 | bytes 46137348 | tf_op jit(solution)/shard_map/while/body/eval_jaxpr/tab,tbr->tar/dot_general | solution.py:30
  220.7 24.3 %scatter_fusion = f32[16,128,256]{2,1,0:T(8,128)S(1)} fusion(f32[16,128,256]{2,1,0:T(8,128)S(1)} %get-tuple-element.205, s32[128]{0:T(128)S(1)} %get-tuple-element.191, f32[128,128,256]{2,1,0:T(8,128)} %fusion.20), kind=kCustom, calls=%fused_computation.2.clone.1 | custom fusion | flops 4194304 | bytes 50332160 | tf_op jit(solution)/shard_map/while/body/eval_jaxpr/scatter-add | solution.py:31
  245.9 7.8 %gather_fusion.1 = bf16[128,128,256]{2,1,0:T(8,128)(2,1)} fusion(bf16[16,128,256]{2,1,0:T(8,128)(2,1)} %get-tuple-element.219, s32[1024]{0:T(1024)S(1)} %pad_clamp_fusion.5), kind=kCustom, calls=%fused_computation.clone.1 | custom fusion | bytes 16777728 | tf_op jit(solution)/shard_map/while/body/eval_jaxpr/gather | solution.py:23
  253.7 9.9 %gather_fusion = bf16[128,128,256]{2,1,0:T(8,128)(2,1)} fusion(bf16[128,128,256]{2,1,0:T(8,128)(2,1)} %get-tuple-element.221, s32[1024]{0:T(1024)S(1)} %pad_clamp_fusion.4), kind=kCustom, calls=%fused_computation.1.clone.1 | custom fusion | bytes 16777728 | tf_op jit(solution)/shard_map/while/body/eval_jaxpr/gather | solution.py:45
  263.6 17.4 %fusion.20 = f32[128,128,256]{2,1,0:T(8,128)} fusion(bf16[128,128,256]{2,1,0:T(8,128)(2,1)} %gather_fusion, bf16[512,128,128]{2,1,0:T(8,128)(2,1)} %get-tuple-element.218, s32[]{:T(128)S(6)} %select_n.29, bf16[128,128,256]{2,1,0:T(8,128)(2,1)} %gather_fusion.1), kind=kOutput, calls=%fused_computation.4.clone.1 | convolution fusion | flops 2155872256 | bytes 46137348 | tf_op jit(solution)/shard_map/while/body/eval_jaxpr/tab,tbr->tar/dot_general | solution.py:30
  281.0 24.4 %scatter_fusion = f32[16,128,256]{2,1,0:T(8,128)S(1)} fusion(f32[16,128,256]{2,1,0:T(8,128)S(1)} %get-tuple-element.205, s32[128]{0:T(128)S(1)} %get-tuple-element.191, f32[128,128,256]{2,1,0:T(8,128)} %fusion.20), kind=kCustom, calls=%fused_computation.2.clone.1 | custom fusion | flops 4194304 | bytes 50332160 | tf_op jit(solution)/shard_map/while/body/eval_jaxpr/scatter-add | solution.py:31
  306.2 7.8 %gather_fusion.1 = bf16[128,128,256]{2,1,0:T(8,128)(2,1)} fusion(bf16[16,128,256]{2,1,0:T(8,128)(2,1)} %get-tuple-element.219, s32[1024]{0:T(1024)S(1)} %pad_clamp_fusion.5), kind=kCustom, calls=%fused_computation.clone.1 | custom fusion | bytes 16777728 | tf_op jit(solution)/shard_map/while/body/eval_jaxpr/gather | solution.py:23
  313.9 9.9 %gather_fusion = bf16[128,128,256]{2,1,0:T(8,128)(2,1)} fusion(bf16[128,128,256]{2,1,0:T(8,128)(2,1)} %get-tuple-element.221, s32[1024]{0:T(1024)S(1)} %pad_clamp_fusion.4), kind=kCustom, calls=%fused_computation.1.clone.1 | custom fusion | bytes 16777728 | tf_op jit(solution)/shard_map/while/body/eval_jaxpr/gather | solution.py:45
  323.9 17.4 %fusion.20 = f32[128,128,256]{2,1,0:T(8,128)} fusion(bf16[128,128,256]{2,1,0:T(8,128)(2,1)} %gather_fusion, bf16[512,128,128]{2,1,0:T(8,128)(2,1)} %get-tuple-element.218, s32[]{:T(128)S(6)} %select_n.29, bf16[128,128,256]{2,1,0:T(8,128)(2,1)} %gather_fusion.1), kind=kOutput, calls=%fused_computation.4.clone.1 | convolution fusion | flops 2155872256 | bytes 46137348 | tf_op jit(solution)/shard_map/while/body/eval_jaxpr/tab,tbr->tar/dot_general | solution.py:30
  341.3 24.3 %scatter_fusion = f32[16,128,256]{2,1,0:T(8,128)S(1)} fusion(f32[16,128,256]{2,1,0:T(8,128)S(1)} %get-tuple-element.205, s32[128]{0:T(128)S(1)} %get-tuple-element.191, f32[128,128,256]{2,1,0:T(8,128)} %fusion.20), kind=kCustom, calls=%fused_computation.2.clone.1 | custom fusion | flops 4194304 | bytes 50332160 | tf_op jit(solution)/shard_map/while/body/eval_jaxpr/scatter-add | solution.py:31
  365.7 1.3 copy-done
  367.6 10.1 %convert_reduce_fusion = f32[512,128]{1,0:T(8,128)S(1)} fusion(bf16[1,1,512,128,128]{4,3,2,1,0:T(8,128)(2,1)} %bitcast.25), kind=kLoop, calls=%fused_computation.14 | loop fusion | flops 16711680 | bytes 17039360 | tf_op jit(solution)/shard_map/reduce_sum | solution.py:48
  378.2 6.7 %all-reduce = f32[2048,2]{0,1:T(2,128)S(1)} all-reduce(f32[2048,2]{0,1:T(2,128)S(1)} %broadcast_in_dim.28), channel_id=3, replica_groups=mesh['fiber'=2,'blk'=64] {'fiber'}, use_global_device_ids=true, to_apply=%region_5.0.clone | all-reduce | flops 4096 | bytes 32768
  385.6 12.6 %reduce-scatter.2.cloned.1.call-done = f32[2048,128]{1,0:T(8,128)} async-done(((f32[2048,256]{1,0:T(8,128)}), f32[2048,128]{1,0:T(8,128)}) %reduce-scatter.2.cloned.1.call-update) | async-done | bytes 1048592 | tf_op jit(solution)/shard_map/reduce_scatter | solution.py:56
  398.2 2.4 multiply_convert_fusion.2
  (28 shorter events, 6.6 us)
Async XLA Ops:
  6.5 29.6 %all-gather.3.cloned.1.call-start = ((), (), s32[]{:S(2)}) async-start(), calls=%async_computation.1 | async-start | bytes 1572864 | tf_op jit(solution)/shard_map/all_gather | solution.py:10
  7.3 117.1 %all-gather.5.cloned.1.call-start = ((), (), s32[]{:S(2)}) async-start(), calls=%async_computation.2 | async-start | bytes 8519680 | tf_op jit(solution)/shard_map/all_gather | solution.py:34
  8.0 390.2 %reduce-scatter.2.cloned.1.call-start = ((), (), s32[]{:S(2)}) async-start(), calls=%async_computation.3 | async-start | bytes 3145728 | tf_op jit(solution)/shard_map/reduce_scatter | solution.py:56
  124.6 242.5 %copy-start.2 = (u32[128]{0:T(128)S(1)}, u32[128]{0:T(128)}, u32[]{:S(2)}) copy-start(u32[128]{0:T(128)} %constant.54) | copy-start | bytes 1540
  365.7 1.3 copy-start
  367.6 10.1 %copy-start.1 = (s32[512]{0:T(512)S(1)}, s32[512]{0:T(512)}, u32[]{:S(2)}) copy-start(s32[512]{0:T(512)} %get-tuple-element.239) | copy-start | bytes 6148
Sparse Core Ops, SparseCore 0:
  9.0 27.0 all-gather.2
  39.2 85.0 all-gather.4
  367.1 31.0 reduce-scatter.1
where the time goes:
time: 409 us; the launch traced here: 407 us
  waiting for transfers between devices  130 us (32%)
  other arithmetic  114 us (28%)
  local copies, waits for them, and re-layouts  73 us (18%)
  matrix products  70 us (17%)
  between operations  13.2 us (3%)
  blocking collectives  6.69 us (2%)
    scatter-add x4, other arithmetic, accumulate(): return totals.at[user_ids].add(products)  97.4 us
    all_gather x1, waiting for transfers between devices, shards(): lax.all_gather(items, 'blk', axis=0, tiled=True)  88.2 us
    dot_general x4, matrix products, accumulate(): jnp.einsum('tab,tbr->tar', weight, item_rows, preferred_element_type=jnp....  69.6 us
    gather x4, local copies, waits for them, and re-layouts, one_group(): gathered[item_ids]  39.8 us
    gather x4, local copies, waits for them, and re-layouts, accumulate(): user_rows = panel_blocks[user_ids]  31 us
    all_gather x1, waiting for transfers between devices, shards(): panel_rows = lax.all_gather(users, 'fiber', axis=1, tiled=True)  28.1 us
    reduce_scatter x1, waiting for transfers between devices, shards(): lax.psum_scatter(totals.reshape(-1, rank_width), 'fiber', scatter_dimensi...  12.6 us
    reduce_sum x1, other arithmetic, shards(): row_sums = jnp.sum(conf_tiles, axis=-1, dtype=jnp.float32)  10.1 us
  transfers between devices with their start and end apart: 3, of which 3 were waited for; matrix products, arithmetic and copies ran while one was open for 3% of the time, Pallas kernels for 0%

commit v1 on v0

v1 whole, which is shorter than its diff:
```python
import functools

import jax
import jax.numpy as jnp
from jax import lax
from jax.experimental import pallas as pl
from jax.experimental.pallas import tpu as pltpu
from jax.sharding import PartitionSpec as P

MESH = pl.DeviceIdType.MESH
TB = 128
UB = 16
IB = 128
T = 512
R = 256
G = 4
SLOTS = 640


def order_tiles(tu_ref, ti_ref, perm_ref):
    users = tu_ref[...]
    owner = lax.broadcasted_iota(jnp.int32, (UB, T), 0) == users
    hot = owner.astype(jnp.float32).astype(jnp.bfloat16)
    before = lax.broadcasted_iota(jnp.int32, (T, T), 0) < lax.broadcasted_iota(jnp.int32, (T, T), 1)
    rank = jnp.dot(hot, before.astype(jnp.float32).astype(jnp.bfloat16), preferred_element_type=jnp.float32)
    count = jnp.sum(owner.astype(jnp.float32), axis=1, keepdims=True)
    steps = jnp.floor((count + (G - 1)) * (1.0 / G))
    earlier = lax.broadcasted_iota(jnp.int32, (UB, TB), 0)
    start = jnp.zeros((UB, 1), jnp.float32)
    for a in range(UB - 1):
        start = start + jnp.where(earlier[:, :1] > a, steps[a : a + 1, :] * G, 0.0)
    place = jnp.sum(jnp.where(owner, rank + start, 0.0), axis=0, keepdims=True)
    match = lax.broadcasted_iota(jnp.int32, (SLOTS, T), 0) == place.astype(jnp.int32)
    number = lax.broadcasted_iota(jnp.int32, (1, T), 1) + 1
    rows = lax.broadcasted_iota(jnp.int32, (8, T), 0)
    fields = jnp.where(
        rows == 0,
        number // 256,
        jnp.where(rows == 1, number % 256, jnp.where(rows == 2, ti_ref[...], users)),
    )
    found = lax.dot_general(
        fields.astype(jnp.float32).astype(jnp.bfloat16),
        match.astype(jnp.float32).astype(jnp.bfloat16),
        (((1,), (1,)), ((), ())),
        preferred_element_type=jnp.float32,
    )
    packed = found[0:1] * (256.0 * 2048.0) + found[1:2] * 2048.0 + found[2:3] * 16.0 + found[3:4]
    total = jnp.sum(steps, axis=0, keepdims=True)
    out_rows = lax.broadcasted_iota(jnp.int32, (8, SLOTS), 0)
    perm_ref[...] = jnp.where(out_rows == 0, packed, total).astype(jnp.int32)


def gather_kernel(users, items, conf, tu, ti, u_all, v_all, vt_all, c_all, perm, send, recv, local):
    f, b = lax.axis_index("fiber"), lax.axis_index("blk")
    zh, x, y, k = b // 32, (b // 8) % 4, (b // 2) % 4, b % 2
    p, q = x * (1 - k) + y * k, y * (1 - k) + x * k

    def shard(zh_, p_, q_, k_):
        return zh_ * 32 + (p_ * (1 - k_) + q_ * k_) * 8 + (q_ * (1 - k_) + p_ * k_) * 2 + k_

    def zr(r):
        return zh if r == 0 else 1 - zh

    def mine(r, dp, dq):
        return shard(zr(r), (p + dp) % 4, (q + dq) % 4, k)

    def others(r, dp, dq):
        return shard(zr(r), (q + dp) % 4, (p + dq) % 4, 1 - k)

    def dev(blk, fib=f):
        return {"fiber": fib, "blk": blk}

    first = {1: dev(shard(zh, (p + 1) % 4, q, k)), -1: dev(shard(zh, (p + 3) % 4, q, k))}
    second = {1: dev(shard(zh, p, (q + 1) % 4, k)), -1: dev(shard(zh, p, (q + 3) % 4, k))}
    across = dev(shard(1 - zh, p, q, k), 1 - f)
    sibling = dev(b + 1 - 2 * k)
    partner = dev(b, 1 - f)
    around = [first[1], first[-1], second[1], second[-1], across, sibling, partner]

    barrier = pltpu.get_barrier_semaphore()
    for d in around:
        pl.semaphore_signal(barrier, inc=1, device_id=d, device_id_type=MESH)
    pl.semaphore_wait(barrier, len(around))

    def slot(r, dp, dq):
        return r * 16 + (dp % 4) * 4 + dq % 4

    def block(ref, s):
        return ref.at[pl.ds(s * 2, 2)]

    def copy(src, dst, n, d):
        return pltpu.make_async_remote_copy(
            src_ref=src, dst_ref=dst, send_sem=send.at[n], recv_sem=recv.at[n], device_id=d, device_id_type=MESH
        )

    sent = []

    def push(r, dp, dq, to, d, n_dp, n_dq, n_r):
        s = mine(r, dp, dq)
        src = items if (r, dp, dq) == (0, 0, 0) else block(v_all, s)
        c = copy(src, block(v_all, s), slot(n_r, n_dp, n_dq) + to, d)
        c.start()
        sent.append(c)

    def have(r, dp, dq):
        if dp == 0 and dq == 0:
            if r == 0:
                push(r, 0, 0, 0, across, 0, 0, 1)
            push(r, 0, 0, 0, first[1], -1, 0, r)
            push(r, 0, 0, 0, first[-1], 1, 0, r)
        if dq == 0:
            if dp == -1 and r == 0:
                push(r, dp, 0, 0, first[1], -2, 0, r)
            if dp == 1 and r == 1:
                push(r, dp, 0, 0, first[-1], 2, 0, r)
            push(r, dp, 0, 0, second[1], dp, -1, r)
            push(r, dp, 0, 0, second[-1], dp, 1, r)
        if dq == -1 and r == 0:
            push(r, dp, dq, 0, second[1], dp, -2, r)
        if dq == 1 and r == 1:
            push(r, dp, dq, 0, second[-1], dp, 2, r)
        push(r, dp, dq, 32, sibling, dp, dq, r)

    def turn(s):
        for j in range(2):
            vt_all[s * 2 + j] = v_all[s * 2 + j].T

    def arrive(r, dp, dq):
        s = mine(r, dp, dq)
        copy(block(v_all, s), block(v_all, s), slot(r, dp, dq), sibling).wait_recv()
        have(r, dp, dq)
        turn(s)

    def arrive_sibling(r, dp, dq):
        s = others(r, dp, dq)
        copy(block(v_all, s), block(v_all, s), slot(r, dp, dq) + 32, sibling).wait_recv()
        turn(s)

    own = pltpu.make_async_copy(items, block(v_all, b), local.at[0])
    half = pltpu.make_async_copy(users, u_all.at[f], local.at[1])
    tiles = pltpu.make_async_copy(conf, c_all.at[pl.ds(1, T)], local.at[2])
    have(0, 0, 0)
    swap = copy(users, u_all.at[f], 64, partner)
    swap.start()
    own.start()
    half.start()
    tiles.start()
    c_all[0] = jnp.zeros((TB, TB), jnp.bfloat16)
    own.wait()

    groups = [
        [(1, 0, 0)],
        [(0, -1, 0), (0, 1, 0)],
        [(0, 0, -1), (0, 0, 1)],
        [(1, -1, 0), (1, 1, 0)],
        [(1, 0, -1), (1, 0, 1)],
        [(0, -2, 0), (1, 2, 0)],
        [(0, -1, -1), (0, -1, 1), (0, 1, -1), (0, 1, 1)],
        [(0, 0, -2), (1, 0, 2)],
        [(1, -1, -1), (1, -1, 1), (1, 1, -1), (1, 1, 1)],
        [(0, -1, -2), (1, -1, 2), (0, 1, -2), (1, 1, 2)],
        [(0, -2, -1), (0, -2, 1), (1, 2, -1), (1, 2, 1)],
        [(0, -2, -2), (1, 2, 2)],
    ]
    late = [(0, 0, 0)]
    turn(b)
    order_tiles(tu, ti, perm)
    for group in groups:
        for event in group:
            arrive(*event)
        for event in late:
            arrive_sibling(*event)
        late = group
    for event in late:
        arrive_sibling(*event)
    copy(users, u_all.at[1 - f], 64, partner).wait_recv()
    half.wait()
    tiles.wait()
    swap.wait_send()
    for c in sent:
        c.wait_send()


def products_kernel(perm, u_all, v_all, vt_all, c_all, keep_ref, give_ref, weight_ref, totals, sums):
    f = lax.axis_index("fiber")
    totals[...] = jnp.zeros_like(totals)
    sums[...] = jnp.zeros_like(sums)
    steps = perm[1, 0]

    def entry(s, j):
        return perm[0, s * G + j]

    def item(e):
        return lax.shift_right_logical(e, 4) & 127

    def rows(s):
        a = entry(s, 0) & 15
        return pl.ds(pl.multiple_of(a * TB, TB), TB)

    def scoped(a0, a1, b0, b1, p0, p1):
        even, odd, prod = (a0, a1), (b0, b1), (p0, p1)

        def issue(s, acc):
            d = rows(s)
            u = jnp.concatenate([u_all[0, d, :], u_all[1, d, :]], axis=1)
            for m in range(2):
                e0, e1 = entry(s, 2 * m), entry(s, 2 * m + 1)
                vt = jnp.concatenate([vt_all[item(e0)], vt_all[item(e1)]], axis=1)
                pltpu.matmul_push_rhs(vt, 0, m)
                pltpu.matmul_acc_lhs(acc[m], u, load_staged_rhs=0)

        def finish(s, acc):
            d = rows(s)
            entries = [entry(s, j) for j in range(G)]
            weight_sum = None
            for m in range(2):
                e0, e1 = entries[2 * m], entries[2 * m + 1]
                v = jnp.concatenate([v_all[item(e0)], v_all[item(e1)]], axis=0)
                pltpu.matmul_push_rhs(v, 1, m)
            for m in range(2):
                e0, e1 = entries[2 * m], entries[2 * m + 1]
                scores = pltpu.matmul_pop(acc[m])
                c0 = c_all[lax.shift_right_logical(e0, 11)].astype(jnp.float32)
                c1 = c_all[lax.shift_right_logical(e1, 11)].astype(jnp.float32)
                weight = jnp.concatenate([c0, c1], axis=1) * (1.0 - scores)
                pltpu.matmul_acc_lhs(prod[m], weight.astype(jnp.bfloat16), load_staged_rhs=1)
                weight_sum = c0 + c1 if weight_sum is None else weight_sum + (c0 + c1)
            sums[d, :] += weight_sum
            return d

        def flush(d):
            totals[d, :] += pltpu.matmul_pop(prod[0]) + pltpu.matmul_pop(prod[1])

        issue(0, even)

        def two(i, carry):
            issue(2 * i + 1, odd)
            d0 = finish(2 * i, even)
            flush(d0)
            issue(2 * i + 2, even)
            d1 = finish(2 * i + 1, odd)
            flush(d1)
            return carry

        lax.fori_loop(0, (steps + 1) // 2, two, 0)
        for m in range(2):
            pltpu.matmul_pop(even[m])

    acc = [pltpu.ACC(m)((TB, R), jnp.float32) for m in (0, 1, 0, 1, 0, 1)]
    pl.run_scoped(scoped, *acc)

    def out(a, carry):
        d = pl.ds(pl.multiple_of(a * TB, TB), TB)
        t = totals[d, :]
        low, high = t[:, :TB], t[:, TB:]
        keep_ref[d, :] = jnp.where(f == 0, low, high)
        give_ref[d, :] = jnp.where(f == 0, high, low).astype(jnp.bfloat16)
        weight_ref[pl.ds(a, 1), :] = jnp.sum(sums[d, :].T, axis=0, keepdims=True)
        return carry

    lax.fori_loop(0, UB, out, 0)


def combine_kernel(keep, give, weight, out, got, got_weight, send, recv):
    f, b = lax.axis_index("fiber"), lax.axis_index("blk")
    partner = {"fiber": 1 - f, "blk": b}
    barrier = pltpu.get_barrier_semaphore()
    pl.semaphore_signal(barrier, inc=1, device_id=partner, device_id_type=MESH)
    pl.semaphore_wait(barrier, 1)

    def copy(src, dst, n):
        return pltpu.make_async_remote_copy(
            src_ref=src,
            dst_ref=dst,
            send_sem=send.at[n],
            recv_sem=recv.at[n],
            device_id=partner,
            device_id_type=MESH,
        )

    copies = [copy(weight, got_weight, 0)]
    parts, step = 8, UB // 8
    for i in range(parts):
        d = pl.ds(i * step * TB, step * TB)
        copies.append(copy(give.at[d], got.at[d], i + 1))
    for c in copies:
        c.start()
    copies[0].wait_recv()
    scale = lax.rsqrt(1.0 + weight[...] + got_weight[...])
    for i in range(parts):
        copies[i + 1].wait_recv()
        for j in range(step):
            a = i * step + j
            d = pl.ds(a * TB, TB)
            by_row = jnp.broadcast_to(scale[a : a + 1, :], (TB, TB)).T
            out[d, :] = ((keep[d, :] + got[d, :].astype(jnp.float32)) * by_row).astype(jnp.bfloat16)
    for c in copies:
        c.wait_send()


def shards(users, items, tile_users, tile_items, confidence):
    vmem = pl.BlockSpec(memory_space=pltpu.VMEM)
    smem = pl.BlockSpec(memory_space=pltpu.SMEM)
    any_space = pl.BlockSpec(memory_space=pl.ANY)
    bf16, f32 = jnp.bfloat16, jnp.float32
    rows = UB * TB
    u_all, v_all, vt_all, c_all, perm = pl.pallas_call(
        gather_kernel,
        name="gather",
        in_specs=[any_space, any_space, any_space, vmem, vmem],
        out_specs=[vmem, vmem, vmem, vmem, vmem],
        out_shape=(
            pltpu.VMEM((2, rows, TB), bf16),
            pltpu.VMEM((IB, TB, R), bf16),
            pltpu.VMEM((IB, R, TB), bf16),
            pltpu.VMEM((T + 1, TB, TB), bf16),
            jax.ShapeDtypeStruct((8, SLOTS), jnp.int32),
        ),
        scratch_shapes=[
            pltpu.SemaphoreType.DMA((65,)),
            pltpu.SemaphoreType.DMA((65,)),
            pltpu.SemaphoreType.DMA((3,)),
        ],
        compiler_params=pltpu.CompilerParams(collective_id=0, has_side_effects=True, vmem_limit_bytes=8 << 20),
    )(
        users,
        items.reshape(2, TB, R),
        confidence.reshape(T, TB, TB),
        tile_users.reshape(1, T),
        tile_items.reshape(1, T),
    )
    keep, give, weight = pl.pallas_call(
        products_kernel,
        name="products",
        in_specs=[smem, vmem, vmem, vmem, vmem],
        out_specs=[vmem, vmem, vmem],
        out_shape=(
            pltpu.VMEM((rows, TB), f32),
            pltpu.VMEM((rows, TB), bf16),
            pltpu.VMEM((UB, TB), f32),
        ),
        scratch_shapes=[pltpu.VMEM((rows, R), f32), pltpu.VMEM((rows, TB), f32)],
        compiler_params=pltpu.CompilerParams(vmem_limit_bytes=12 << 20),
    )(perm, u_all, v_all, vt_all, c_all)
    return pl.pallas_call(
        combine_kernel,
        name="combine",
        in_specs=[vmem, vmem, vmem],
        out_specs=vmem,
        out_shape=jax.ShapeDtypeStruct((rows, TB), bf16),
        scratch_shapes=[
            pltpu.VMEM((rows, TB), bf16),
            pltpu.VMEM((UB, TB), f32),
            pltpu.SemaphoreType.DMA((9,)),
            pltpu.SemaphoreType.DMA((9,)),
        ],
        compiler_params=pltpu.CompilerParams(collective_id=1, has_side_effects=True, vmem_limit_bytes=8 << 20),
    )(keep, give, weight)


def solution(mesh):
    in_specs = (
        P("blk", "fiber"),
        P("blk", None),
        P("blk", "fiber", None),
        P("blk", "fiber", None),
        P("blk", "fiber", None, None, None),
    )

    def run(*args):
        with jax.sharding.use_abstract_mesh(mesh.abstract_mesh):
            return jax.shard_map(
                shards, mesh=mesh, in_specs=in_specs, out_specs=P("blk", "fiber"), check_vma=False
            )(*args)

    return run
```

time: 409 us -> 88.7 us (0.22)
  waiting for transfers between devices: 130 us -> 0 us
  other arithmetic: 114 us -> 0 us
  Pallas kernels: 0 us -> 84.3 us
  matrix products: 70 us -> 0 us
  local copies, waits for them, and re-layouts: 73 us -> 4.1 us
  between operations: 13.2 us -> 0.03 us
  blocking collectives: 6.69 us -> 0 us
    all_gather x2 -> x0, waiting for transfers between devices: 116 us -> none  [the longest x1 88.2 us: shards(): lax.all_gather(items, 'blk', axis=0, tiled=True)]
    scatter-add x4 -> x0, other arithmetic: 97.4 us -> none  [accumulate(): return totals.at[user_ids].add(products)]
    pallas_call x0 -> x3, Pallas kernels: none -> 84.3 us  [the longest x1 39.3 us: shards(): pl.pallas_call(gather_kernel, name='gather', in_specs=[any_space, any_spa...]
    gather x8 -> x0, local copies, waits for them, and re-layouts: 70.8 us -> none  [the longest x4 39.8 us: one_group(): gathered[item_ids]]
    dot_general x5 -> x0, matrix products: 70 us -> none  [the longest x4 69.6 us: accumulate(): jnp.einsum('tab,tbr->tar', weight, item_rows, preferred_element_type=jnp....]
    reduce_scatter x1 -> x0, waiting for transfers between devices: 12.6 us -> none  [shards(): lax.psum_scatter(totals.reshape(-1, rank_width), 'fiber', scatter_dimensi...]
    reduce_sum x1 -> x0, other arithmetic: 10.1 us -> none  [shards(): row_sums = jnp.sum(conf_tiles, axis=-1, dtype=jnp.float32)]
    unnamed x1 -> x0, blocking collectives: 6.69 us -> none
  transfers between devices with their start and end apart: 3 -> 0, of which waited for: 3 -> 0; matrix products, arithmetic and copies ran while one was open for 3% -> 0% of each run, Pallas kernels for 0% -> 0%
where the time goes in v1:
time: 88.7 us; the launch traced here: 88.5 us
  Pallas kernels  84.3 us (95%)
  local copies, waits for them, and re-layouts  4.1 us (5%)
    pallas_call x1, Pallas kernels, shards(): pl.pallas_call(gather_kernel, name='gather', in_specs=[any_space, any_spa...  39.3 us
    pallas_call x1, Pallas kernels, shards(): pl.pallas_call(products_kernel, name='products', in_specs=[smem, vmem, vm...  31.3 us
    pallas_call x1, Pallas kernels, shards(): pl.pallas_call(combine_kernel, name='combine', in_specs=[vmem, vmem, vmem...  13.7 us
    unnamed x9, local copies, waits for them, and re-layouts  4.1 us

profile of v1, /device:TPU:1, one launch (start us, length us, event | category | flops | bytes accessed | tf_op | source)
XLA Modules:
  0.0 88.5 jit_solution(6667077078784947413)
XLA Ops:
  0.0 0.0 copy-start
  0.0 1.0 %copy-done = bf16[2048,128]{1,0:T(8,128)(2,1)S(1)} copy-done((bf16[2048,128]{1,0:T(8,128)(2,1)S(1)}, bf16[2048,128]{1,0:T(8,128)(2,1)}, u32[]{:S(2)}) %copy-start) | copy-done | bytes 524312
  1.0 0.0 copy-start.1
  1.0 0.9 %copy-done.1 = bf16[256,256]{1,0:T(8,128)(2,1)S(1)} copy-done((bf16[256,256]{1,0:T(8,128)(2,1)S(1)}, bf16[256,256]{1,0:T(8,128)(2,1)}, u32[]{:S(2)}) %copy-start.1) | copy-done | bytes 131096
  1.9 0.0 copy-start.2
  1.9 0.7 copy-done.2
  2.6 0.0 copy-start.3
  2.6 0.7 copy-done.3
  3.3 39.3 %gather.1 = (bf16[2,2048,128]{2,1,0:T(8,128)(2,1)S(1)}, bf16[128,128,256]{2,1,0:T(8,128)(2,1)S(1)}, bf16[128,256,128]{2,1,0:T(8,128)(2,1)S(1)}, bf16[513,128,128]{2,1,0:T(8,128)(2,1)S(1)}, s32[8,640]{1,0:T(8,128)S(1)}) custom-call(bf16[2048,128]{1,0:T(8,128)(2,1)S(1)} %copy-done, bf16[2,128,256]{2,1,0:T(8,128)(2,1)S(1)} %bitcast.4, ...), custom_call_target="tpu_custom_call" | custom-call | tf_op jit(solution)/shard_map/gather/pallas_call | solution.py:307
  42.7 31.3 %products.1 = (f32[2048,128]{1,0:T(8,128)S(1)}, bf16[2048,128]{1,0:T(8,128)(2,1)S(1)}, f32[16,128]{1,0:T(8,128)S(1)}) custom-call(s32[8,640]{1,0:T(8,128)S(1)} %get-tuple-element.13.perm, bf16[2,2048,128]{2,1,0:T(8,128)(2,1)S(1)} %get-tuple-element.14.u_all, bf16[128,128,256]{2,1,0:T(8,128)(2,1)S(1)} %get-tuple-element.15.v_all, ...), custom_call_target="tpu_custom_call" | custom-call | tf_op jit(solution)/shard_map/products/pallas_call | solution.py:332
  74.0 13.7 %combine.1 = bf16[2048,128]{1,0:T(8,128)(2,1)S(1)} custom-call(f32[2048,128]{1,0:T(8,128)S(1)} %get-tuple-element.18.keep, bf16[2048,128]{1,0:T(8,128)(2,1)S(1)} %get-tuple-element.19.give, f32[16,128]{1,0:T(8,128)S(1)} %get-tuple-element.20.weight), custom_call_target="tpu_custom_call" | custom-call | tf_op jit(solution)/shard_map/combine/pallas_call | solution.py:345
  87.7 0.8 copy.7
Async XLA Ops:
  0.0 1.0 %copy-start = (bf16[2048,128]{1,0:T(8,128)(2,1)S(1)}, bf16[2048,128]{1,0:T(8,128)(2,1)}, u32[]{:S(2)}) copy-start(bf16[2048,128]{1,0:T(8,128)(2,1)} %users.1) | copy-start | bytes 1572868
  1.0 0.9 %copy-start.1 = (bf16[256,256]{1,0:T(8,128)(2,1)S(1)}, bf16[256,256]{1,0:T(8,128)(2,1)}, u32[]{:S(2)}) copy-start(bf16[256,256]{1,0:T(8,128)(2,1)} %param.6) | copy-start | bytes 393220
  1.9 0.7 copy-start.2
  2.6 0.7 copy-start.3

commit v2 on v0

v2 whole, which is shorter than its diff:
```python
import functools

import jax
import jax.numpy as jnp
from jax import lax
from jax.experimental import pallas as pl
from jax.experimental.pallas import tpu as pltpu
from jax.sharding import PartitionSpec as P

MESH = pl.DeviceIdType.MESH
TB = 128
UB = 16
IB = 128
T = 512
R = 256
G = 4
DEEP, AHEAD, BEHIND = 4, 3, 2
NC = 4
CB = UB // NC
LAG = 6
SWAPS = 4
EXTRA = 16
SLOTS = 640

PLAN = (
    (0, 0, 0, 1, "M"), (0, 0, -1, 0, "P"), (1, 1, 0, 0, "A"), (0, 0, 0, -1, "P"), (0, 0, 1, 0, "M"),
    (0, 1, 0, 1, "M"), (0, 1, 0, -1, "P"), (1, 0, 0, 0, "A"), (0, 1, -1, 0, "P"), (0, 1, 1, 0, "M"),
    (0, 0, -1, 1, "p"), (0, 0, 0, 2, "M"), (1, 1, -1, 0, "A"), (0, 0, 1, 1, "m"), (0, 0, -1, -1, "P"),
    (0, 0, 2, 0, "P"), (1, 1, 1, 0, "M"), (1, 0, 0, 1, "A"), (1, 1, 0, -1, "P"), (0, 0, 1, -1, "m"),
    (0, 1, 1, 1, "m"), (1, 0, -1, 0, "P"), (0, 1, -1, 1, "F"), (1, 0, 0, -1, "A"), (0, 1, 1, -1, "m"),
    (0, 1, 2, 0, "P"), (1, 0, 1, 0, "M"), (0, 0, -1, 2, "P"), (0, 1, 0, 2, "F"), (1, 1, -1, 1, "A"),
    (0, 0, 1, 2, "M"), (0, 0, 2, -1, "p"), (0, 0, 2, 1, "M"), (1, 1, -1, -1, "p"), (0, 1, -1, -1, "F"),
    (1, 0, 1, 1, "m"), (1, 0, 2, 0, "P"), (1, 1, 1, 1, "A"), (1, 1, 1, -1, "m"), (1, 0, -1, -1, "P"),
    (1, 1, 0, 1, "F"), (0, 1, 2, 1, "p"), (0, 1, -1, 2, "M"), (1, 1, 2, 0, "A"), (1, 0, 1, -1, "m"),
    (0, 0, 2, 2, "p"), (0, 1, 1, 2, "m"), (0, 1, 2, -1, "p"), (1, 0, -1, 1, "A"), (1, 1, -1, 2, "M"),
    (1, 0, 2, -1, "P"), (1, 1, 2, 1, "m"), (1, 1, 1, 2, "P"), (1, 0, 0, 2, "A"), (1, 1, 2, -1, "m"),
    (1, 0, -1, 2, "P"), (1, 1, 0, 2, "M"), (1, 0, 1, 2, "P"), (1, 0, 2, 1, "A"), (0, 1, 2, 2, "M"),
    (1, 0, 2, 2, "P"), (1, 1, 2, 2, "m"),
)


def order_tiles(tu_ref, ti_ref, perm_ref):
    users = tu_ref[...]
    owner = lax.broadcasted_iota(jnp.int32, (UB, T), 0) == users
    hot = owner.astype(jnp.float32).astype(jnp.bfloat16)
    before = lax.broadcasted_iota(jnp.int32, (T, T), 0) < lax.broadcasted_iota(jnp.int32, (T, T), 1)
    rank = jnp.dot(hot, before.astype(jnp.float32).astype(jnp.bfloat16), preferred_element_type=jnp.float32)
    count = jnp.sum(owner.astype(jnp.float32), axis=1, keepdims=True)
    steps = jnp.floor((count + (G - 1)) * (1.0 / G))
    block = lax.broadcasted_iota(jnp.int32, (UB, 1), 0)
    lane = lax.broadcasted_iota(jnp.int32, (1, SLOTS), 1)
    start = jnp.zeros((UB, 1), jnp.float32)
    marks = jnp.zeros((1, SLOTS), jnp.float32)
    base = jnp.zeros((1, 1), jnp.float32)
    for c in range(NC):
        marks = marks + jnp.where(lane == c, base, 0.0)
        inside = base
        for a in range(c * CB, (c + 1) * CB):
            start = start + jnp.where(block == a, inside * G, 0.0)
            inside = inside + steps[a : a + 1, :]
        rounds = jnp.maximum(jnp.floor((inside - base + (DEEP - 1)) * (1.0 / DEEP)), 1.0)
        base = base + rounds * DEEP
    marks = marks + jnp.where(lane == NC, base, 0.0)
    place = jnp.sum(jnp.where(owner, rank + start, 0.0), axis=0, keepdims=True)
    match = lax.broadcasted_iota(jnp.int32, (SLOTS, T), 0) == place.astype(jnp.int32)
    number = lax.broadcasted_iota(jnp.int32, (1, T), 1) + 1
    rows = lax.broadcasted_iota(jnp.int32, (8, T), 0)
    fields = jnp.where(
        rows == 0,
        number // 256,
        jnp.where(rows == 1, number % 256, jnp.where(rows == 2, ti_ref[...], users)),
    )
    found = lax.dot_general(
        fields.astype(jnp.float32).astype(jnp.bfloat16),
        match.astype(jnp.float32).astype(jnp.bfloat16),
        (((1,), (1,)), ((), ())),
        preferred_element_type=jnp.float32,
    )
    packed = found[0:1] * (256.0 * 2048.0) + found[1:2] * 2048.0 + found[2:3] * 16.0 + found[3:4]
    out_rows = lax.broadcasted_iota(jnp.int32, (8, SLOTS), 0)
    perm_ref[...] = jnp.where(out_rows == 0, packed, marks).astype(jnp.int32)


def source(unit):
    z, h, dp, dq, via = unit
    if via == "A":
        return 0, 1 - h, dp, dq
    if via == "F":
        return z, 1 - h, dp, dq
    back = 1 if via in "Pp" else -1
    if dq and via in "PM":
        dq = (dq + back + 1) % 4 - 1
    else:
        dp = (dp + back + 1) % 4 - 1
    return z, h, dp, dq


def gather_kernel(users, items, conf, tile_users, tile_items, u_all, v_all, vt_all, c_all, perm, tu, ti, send, recv, local):
    f, b = lax.axis_index("fiber"), lax.axis_index("blk")
    zh, x, y, k = b // 32, (b // 8) % 4, (b // 2) % 4, b % 2
    p, q = x * (1 - k) + y * k, y * (1 - k) + x * k

    def shard(zh_, p_, q_, k_):
        return zh_ * 32 + (p_ * (1 - k_) + q_ * k_) * 8 + (q_ * (1 - k_) + p_ * k_) * 2 + k_

    def mine(z, h, dp, dq):
        return shard(zh if z == 0 else 1 - zh, (p + dp) % 4, (q + dq) % 4, k) * 2 + (f + h) % 2

    def others(z, h, dp, dq):
        return shard(zh if z == 0 else 1 - zh, (q + dp) % 4, (p + dq) % 4, 1 - k) * 2 + (f + h) % 2

    def dev(blk, fib=f):
        return {"fiber": fib, "blk": blk}

    first = {"P": dev(shard(zh, (p + 1) % 4, q, k)), "M": dev(shard(zh, (p + 3) % 4, q, k))}
    second = {"P": dev(shard(zh, p, (q + 1) % 4, k)), "M": dev(shard(zh, p, (q + 3) % 4, k))}
    across = dev(shard(1 - zh, p, q, k), 1 - f)
    sibling = dev(b + 1 - 2 * k)
    partner = dev(b, 1 - f)
    around = [first["P"], first["M"], second["P"], second["M"], across, sibling, partner]

    barrier = pltpu.get_barrier_semaphore()
    for d in around:
        pl.semaphore_signal(barrier, inc=1, device_id=d, device_id_type=MESH)
    pl.semaphore_wait(barrier, len(around))

    def slot(z, h, dp, dq):
        return z * 32 + h * 16 + (dp % 4) * 4 + dq % 4

    def copy(src, dst, n, d):
        return pltpu.make_async_remote_copy(
            src_ref=src, dst_ref=dst, send_sem=send.at[n], recv_sem=recv.at[n], device_id=d, device_id_type=MESH
        )

    def target(unit):
        dq, via = unit[3:]
        if via == "A":
            return across
        if via == "F":
            return partner
        return (second if dq and via in "PM" else first)[via.upper()]

    children = {}
    for unit in reversed(PLAN):
        children.setdefault(source(unit), []).append(unit)

    def weight(unit):
        return 1 + sum(weight(c[:4]) for c in children.get(unit, ()))

    sent = []

    def have(unit):
        n = mine(*unit)
        src = items.at[(f + unit[1]) % 2] if unit[0] == unit[2] == unit[3] == 0 else v_all.at[n]
        for c in sorted(children.get(unit, ()), key=lambda c: -weight(c[:4])):
            sent.append(copy(src, v_all.at[n], slot(*c[:4]), target(c)))
            sent[-1].start()
        sent.append(copy(src, v_all.at[n], slot(*unit) + 64, sibling))
        sent[-1].start()

    def turn(n):
        vt_all[n] = v_all[n].T

    swaps = []

    def swap(i):
        d = pl.ds(i * (UB * TB // SWAPS), UB * TB // SWAPS)
        swaps.append((copy(users.at[d], u_all.at[f, d], 128 + i, partner), copy(users.at[d], u_all.at[1 - f, d], 128 + i, partner)))
        swaps[-1][0].start()

    own = pltpu.make_async_copy(items, v_all.at[pl.ds(b * 2, 2)], local.at[0])
    half = pltpu.make_async_copy(users, u_all.at[f], local.at[1])
    tiles = pltpu.make_async_copy(conf, c_all.at[pl.ds(1, T)], local.at[2])
    lists = [
        pltpu.make_async_copy(tile_users, tu, local.at[3]),
        pltpu.make_async_copy(tile_items, ti, local.at[4]),
    ]
    for h in range(2):
        have((0, h, 0, 0))
    swap(0)
    own.start()
    for c in lists:
        c.start()
    half.start()
    tiles.start()
    c_all[0] = jnp.zeros((TB, TB), jnp.bfloat16)

    def own_work():
        own.wait()
        for j in range(2):
            turn(b * 2 + j)
        for c in lists:
            c.wait()
        order_tiles(tu, ti, perm)

    order = [u[:4] for u in PLAN]
    late = [(0, h, 0, 0) for h in range(2)] + order
    for i in range(len(order) + LAG):
        if i < len(order):
            unit = order[i]
            n = mine(*unit)
            copy(v_all.at[n], v_all.at[n], slot(*unit), sibling).wait_recv()
            have(unit)
            turn(n)
            if i == 30:
                own_work()
            if i % 8 == 7 and len(swaps) < SWAPS:
                swap(len(swaps))
        if i >= LAG - 2:
            unit = late[i - (LAG - 2)]
            n = others(*unit)
            copy(v_all.at[n], v_all.at[n], slot(*unit) + 64, sibling).wait_recv()
            turn(n)
    half.wait()
    tiles.wait()
    for out, into in swaps:
        into.wait_recv()
        out.wait_send()
    for c in sent:
        c.wait_send()


def products_kernel(chunk, perm, u_all, v_all, vt_all, c_all, keep_ref, give_ref, weight_ref, totals, sums):
    f = lax.axis_index("fiber")
    totals[...] = jnp.zeros_like(totals)
    sums[...] = jnp.zeros_like(sums)
    begin = perm[1, chunk]
    rounds = (perm[1, chunk + 1] - begin) // DEEP

    def entry(s, j):
        return perm[0, (begin + s) * G + j]

    def item(e):
        return lax.shift_right_logical(e, 4) & 127

    def rows(s, first=0):
        a = jnp.maximum((entry(s, 0) & 15) - first, 0)
        return pl.ds(pl.multiple_of(a * TB, TB), TB)

    def scoped(*accs):
        scores_acc = [(accs[2 * n], accs[2 * n + 1]) for n in range(DEEP)]
        prod_acc = [(accs[2 * n], accs[2 * n + 1]) for n in range(DEEP, 2 * DEEP)]

        def issue(s, r):
            d = rows(s)
            u = jnp.concatenate([u_all[0, d, :], u_all[1, d, :]], axis=1)
            for m in range(2):
                e0, e1 = entry(s, 2 * m), entry(s, 2 * m + 1)
                vt = jnp.concatenate([vt_all[item(e0)], vt_all[item(e1)]], axis=1)
                pltpu.matmul_push_rhs(vt, 0, m)
                pltpu.matmul_acc_lhs(scores_acc[r % DEEP][m], u, load_staged_rhs=0)

        def finish(s, r):
            d = rows(s, chunk * CB)
            entries = [entry(s, j) for j in range(G)]
            weight_sum = None
            for m in range(2):
                e0, e1 = entries[2 * m], entries[2 * m + 1]
                v = jnp.concatenate([v_all[item(e0)], v_all[item(e1)]], axis=0)
                pltpu.matmul_push_rhs(v, 1, m)
                scores = pltpu.matmul_pop(scores_acc[r % DEEP][m])
                c0 = c_all[lax.shift_right_logical(e0, 11)].astype(jnp.float32)
                c1 = c_all[lax.shift_right_logical(e1, 11)].astype(jnp.float32)
                weight = jnp.concatenate([c0, c1], axis=1) * (1.0 - scores)
                pltpu.matmul_acc_lhs(prod_acc[r % DEEP][m], weight.astype(jnp.bfloat16), load_staged_rhs=1)
                weight_sum = c0 + c1 if weight_sum is None else weight_sum + (c0 + c1)
            sums[d, :] += weight_sum

        def flush(s, r):
            low, high = prod_acc[r % DEEP]
            totals[rows(s, chunk * CB), :] += pltpu.matmul_pop(low) + pltpu.matmul_pop(high)

        def stage(s, r, first=False):
            issue(s + AHEAD, r + AHEAD)
            if not first:
                flush(s - BEHIND, r + DEEP - BEHIND)
            finish(s, r)

        for r in range(AHEAD):
            issue(r, r)
        for r in range(DEEP):
            stage(r, r, r < BEHIND)

        def several(i, carry):
            for r in range(DEEP):
                stage(i * DEEP + r, r)
            return carry

        lax.fori_loop(1, rounds, several, 0)
        for r in range(BEHIND):
            flush(rounds * DEEP - BEHIND + r, DEEP - BEHIND + r)
        for r in range(AHEAD):
            for m in range(2):
                pltpu.matmul_pop(scores_acc[r][m])

    pl.run_scoped(scoped, *[pltpu.ACC(n % 2)((TB, R), jnp.float32) for n in range(4 * DEEP)])

    sums_row = []
    for a in range(CB):
        d = pl.ds(a * TB, TB)
        t = totals[d, :]
        low, high = t[:, :TB], t[:, TB:]
        keep_ref[d, :] = jnp.where(f == 0, low, high)
        give_ref[d, :] = jnp.where(f == 0, high, low).astype(jnp.bfloat16)
        sums_row.append(jnp.sum(sums[d, :].T, axis=0, keepdims=True))
    weight = jnp.concatenate(sums_row, axis=0)
    weight_ref[...] = weight
    rest, parts = weight, []
    for _ in range(3):
        parts.append(rest.astype(jnp.bfloat16).astype(jnp.float32))
        rest = rest - parts[-1]
    parts.append(jnp.zeros((EXTRA - 3 * CB, TB), jnp.float32))
    give_ref[CB * TB :, :] = jnp.concatenate(parts, axis=0).astype(jnp.bfloat16)


def combine_kernel(*refs):
    out = refs[-1]
    for c in range(NC):
        keep, got, weight = refs[3 * c : 3 * c + 3]
        sent = got[CB * TB :, :].astype(jnp.float32)
        total = weight[...] + (sent[:CB] + (sent[CB : 2 * CB] + sent[2 * CB : 3 * CB]))
        scale = lax.rsqrt(1.0 + total)
        for a in range(CB):
            d = pl.ds(a * TB, TB)
            by_row = jnp.broadcast_to(scale[a : a + 1, :], (TB, TB)).T
            row = (keep[d, :] + got[d, :].astype(jnp.float32)) * by_row
            out[pl.ds((c * CB + a) * TB, TB), :] = row.astype(jnp.bfloat16)


def shards(users, items, tile_users, tile_items, confidence):
    vmem = pl.BlockSpec(memory_space=pltpu.VMEM)
    smem = pl.BlockSpec(memory_space=pltpu.SMEM)
    hbm = pl.BlockSpec(memory_space=pltpu.HBM)
    bf16, f32 = jnp.bfloat16, jnp.float32
    rows = UB * TB
    u_all, v_all, vt_all, c_all, perm = pl.pallas_call(
        gather_kernel,
        name="gather",
        in_specs=[hbm] * 5,
        out_specs=[vmem, vmem, vmem, vmem, vmem],
        out_shape=(
            pltpu.VMEM((2, rows, TB), bf16),
            pltpu.VMEM((IB, TB, R), bf16),
            pltpu.VMEM((IB, R, TB), bf16),
            pltpu.VMEM((T + 1, TB, TB), bf16),
            jax.ShapeDtypeStruct((8, SLOTS), jnp.int32),
        ),
        scratch_shapes=[
            pltpu.VMEM((1, T), jnp.int32),
            pltpu.VMEM((1, T), jnp.int32),
            pltpu.SemaphoreType.DMA((128 + SWAPS,)),
            pltpu.SemaphoreType.DMA((128 + SWAPS,)),
            pltpu.SemaphoreType.DMA((5,)),
        ],
        compiler_params=pltpu.CompilerParams(collective_id=0, has_side_effects=True, vmem_limit_bytes=8 << 20),
    )(
        *[
            pltpu.with_memory_space_constraint(z, pltpu.HBM)
            for z in (
                users,
                items.reshape(2, TB, R),
                confidence.reshape(T, TB, TB),
                tile_users.reshape(1, T),
                tile_items.reshape(1, T),
            )
        ]
    )
    tiles = T // NC
    parts = []
    for chunk in range(NC):
        keep, give, weight = pl.pallas_call(
            functools.partial(products_kernel, chunk),
            name="products",
            in_specs=[smem, vmem, vmem, vmem, vmem],
            out_specs=[vmem, vmem, vmem],
            out_shape=(
                pltpu.VMEM((CB * TB, TB), f32),
                pltpu.VMEM((CB * TB + EXTRA, TB), bf16),
                pltpu.VMEM((CB, TB), f32),
            ),
            scratch_shapes=[pltpu.VMEM((CB * TB, R), f32), pltpu.VMEM((CB * TB, TB), f32)],
            cost_estimate=pl.CostEstimate(
                flops=tiles * 4 * TB * TB * R, bytes_accessed=tiles * TB * TB * 8, transcendentals=0
            ),
            compiler_params=pltpu.CompilerParams(vmem_limit_bytes=8 << 20),
        )(perm, u_all, v_all, vt_all, c_all)
        parts += [keep, lax.ppermute(give, "fiber", [(0, 1), (1, 0)]), weight]
    return pl.pallas_call(
        combine_kernel,
        name="combine",
        in_specs=[vmem] * len(parts),
        out_specs=vmem,
        out_shape=jax.ShapeDtypeStruct((rows, TB), bf16),
        compiler_params=pltpu.CompilerParams(vmem_limit_bytes=8 << 20),
    )(*parts)


def solution(mesh):
    in_specs = (
        P("blk", "fiber"),
        P("blk", None),
        P("blk", "fiber", None),
        P("blk", "fiber", None),
        P("blk", "fiber", None, None, None),
    )

    def run(*args):
        with jax.sharding.use_abstract_mesh(mesh.abstract_mesh):
            return jax.shard_map(
                shards, mesh=mesh, in_specs=in_specs, out_specs=P("blk", "fiber"), check_vma=False
            )(*args)

    return run
```

time: 409 us -> 64.6 us (0.16)
  waiting for transfers between devices: 130 us -> 3.87 us
  other arithmetic: 114 us -> 0 us
  local copies, waits for them, and re-layouts: 73 us -> 0 us
  matrix products: 70 us -> 0 us
  Pallas kernels: 0 us -> 55.9 us
  between operations: 13.2 us -> 0.05 us
  blocking collectives: 6.69 us -> 0 us
  starting transfers between devices: 0.08 us -> 4.45 us
    all_gather x2 -> x0, waiting for transfers between devices: 116 us -> none  [the longest x1 88.2 us: shards(): lax.all_gather(items, 'blk', axis=0, tiled=True)]
    scatter-add x4 -> x0, other arithmetic: 97.4 us -> none  [accumulate(): return totals.at[user_ids].add(products)]
    gather x8 -> x0, local copies, waits for them, and re-layouts: 70.8 us -> none  [the longest x4 39.8 us: one_group(): gathered[item_ids]]
    dot_general x5 -> x0, matrix products: 70 us -> none  [the longest x4 69.6 us: accumulate(): jnp.einsum('tab,tbr->tar', weight, item_rows, preferred_element_type=jnp....]
    pallas_call x0 -> x6, Pallas kernels: none -> 55.9 us  [the longest x1 35.1 us: shards(): pl.pallas_call(gather_kernel, name='gather', in_specs=[hbm] * 5, out_spec...]
    reduce_scatter x1 -> x0, waiting for transfers between devices: 12.6 us -> none  [shards(): lax.psum_scatter(totals.reshape(-1, rank_width), 'fiber', scatter_dimensi...]
    reduce_sum x1 -> x0, other arithmetic: 10.1 us -> none  [shards(): row_sums = jnp.sum(conf_tiles, axis=-1, dtype=jnp.float32)]
    unnamed x1 -> x0, blocking collectives: 6.69 us -> none
  transfers between devices with their start and end apart: 3 -> 4, of which waited for: 3 -> 1; matrix products, arithmetic and copies ran while one was open for 3% -> 0% of each run, Pallas kernels for 0% -> 24%
where the time goes in v2:
time: 64.6 us; the launch traced here: 64.3 us
  Pallas kernels  55.9 us (87%)
  starting transfers between devices  4.45 us (7%)
  waiting for transfers between devices  3.87 us (6%)
    pallas_call x1, Pallas kernels, shards(): pl.pallas_call(gather_kernel, name='gather', in_specs=[hbm] * 5, out_spec...  35.1 us
    pallas_call x4, Pallas kernels, shards(): pl.pallas_call(functools.partial(products_kernel, chunk), name='products'...  19.6 us
    ppermute x4, starting transfers between devices, shards(): parts += [keep, lax.ppermute(give, 'fiber', [(0, 1), (1, 0)]), weight]  4.45 us
    ppermute x4, waiting for transfers between devices, shards(): parts += [keep, lax.ppermute(give, 'fiber', [(0, 1), (1, 0)]), weight]  3.87 us
  transfers between devices with their start and end apart: 4, of which 1 were waited for; matrix products, arithmetic and copies ran while one was open for 0% of the time, Pallas kernels for 24%

profile of v2, /device:TPU:1, one launch (start us, length us, event | category | flops | bytes accessed | tf_op | source)
XLA Modules:
  0.0 64.3 jit_solution(11500137591434684708)
XLA Ops:
  0.0 35.1 %gather.1 = (bf16[2,2048,128]{2,1,0:T(8,128)(2,1)S(1)}, bf16[128,128,256]{2,1,0:T(8,128)(2,1)S(1)}, bf16[128,256,128]{2,1,0:T(8,128)(2,1)S(1)}, bf16[513,128,128]{2,1,0:T(8,128)(2,1)S(1)}, s32[8,640]{1,0:T(8,128)S(1)}) custom-call(bf16[2048,128]{1,0:T(8,128)(2,1)} %users.1, bf16[2,128,256]{2,1,0:T(8,128)(2,1)} %bitcast.5, bf16[512,128,128]{2,1,0:T(8,128)(2,1)} %bitcast.4, ...), custom_call_target="tpu_custom_call" | custom-call | tf_op jit(solution)/shard_map/gather/pallas_call | solution.py:336
  35.1 4.2 %products.7 = (f32[512,128]{1,0:T(8,128)S(1)}, bf16[528,128]{1,0:T(8,128)(2,1)S(1)}, f32[4,128]{1,0:T(4,128)S(1)}) custom-call(s32[8,640]{1,0:T(8,128)S(1)} %get-tuple-element.22.perm, bf16[2,2048,128]{2,1,0:T(8,128)(2,1)S(1)} %get-tuple-element.23.u_all, bf16[128,128,256]{2,1,0:T(8,128)(2,1)S(1)} %get-tuple-element.24.v_all, ...), custom_call_target="tpu_custom_call" | custom-call | flops 2147483648 | bytes 16777216 | tf_op jit(solution)/shard_map/products/pallas_call | solution.py:371
  39.3 2.7 %collective-permute-start.3 = (bf16[528,128]{1,0:T(8,128)(2,1)S(1)}, bf16[528,128]{1,0:T(8,128)(2,1)S(1)}, u32[]{:S(2)}, u32[]{:S(2)}) collective-permute-start(bf16[528,128]{1,0:T(8,128)(2,1)S(1)} %get-tuple-element.37), channel_id=1, source_target_pairs={{0,64},{64,0},{1,65},{65,1},{2,66},{66,2},{3,67},{67,3},{4,68},{68... | collective-permute-start | bytes 405512 | tf_op jit(solution)/shard_map/ppermute | solution.py:387
  42.1 5.5 %products.6 = (f32[512,128]{1,0:T(8,128)S(1)}, bf16[528,128]{1,0:T(8,128)(2,1)S(1)}, f32[4,128]{1,0:T(4,128)S(1)}) custom-call(s32[8,640]{1,0:T(8,128)S(1)} %get-tuple-element.22.perm, bf16[2,2048,128]{2,1,0:T(8,128)(2,1)S(1)} %get-tuple-element.23.u_all, bf16[128,128,256]{2,1,0:T(8,128)(2,1)S(1)} %get-tuple-element.24.v_all, ...), custom_call_target="tpu_custom_call" | custom-call | flops 2147483648 | bytes 16777216 | tf_op jit(solution)/shard_map/products/pallas_call | solution.py:371
  47.6 0.1 collective-permute-start.2
  47.7 5.0 %products.5 = (f32[512,128]{1,0:T(8,128)S(1)}, bf16[528,128]{1,0:T(8,128)(2,1)S(1)}, f32[4,128]{1,0:T(4,128)S(1)}) custom-call(s32[8,640]{1,0:T(8,128)S(1)} %get-tuple-element.22.perm, bf16[2,2048,128]{2,1,0:T(8,128)(2,1)S(1)} %get-tuple-element.23.u_all, bf16[128,128,256]{2,1,0:T(8,128)(2,1)S(1)} %get-tuple-element.24.v_all, ...), custom_call_target="tpu_custom_call" | custom-call | flops 2147483648 | bytes 16777216 | tf_op jit(solution)/shard_map/products/pallas_call | solution.py:371
  52.6 1.1 %collective-permute-start.1 = (bf16[528,128]{1,0:T(8,128)(2,1)S(1)}, bf16[528,128]{1,0:T(8,128)(2,1)S(1)}, u32[]{:S(2)}, u32[]{:S(2)}) collective-permute-start(bf16[528,128]{1,0:T(8,128)(2,1)S(1)} %get-tuple-element.31), channel_id=1, source_target_pairs={{0,64},{64,0},{1,65},{65,1},{2,66},{66,2},{3,67},{67,3},{4,68},{68... | collective-permute-start | bytes 405512 | tf_op jit(solution)/shard_map/ppermute | solution.py:387
  53.8 5.0 %products.4 = (f32[512,128]{1,0:T(8,128)S(1)}, bf16[528,128]{1,0:T(8,128)(2,1)S(1)}, f32[4,128]{1,0:T(4,128)S(1)}) custom-call(s32[8,640]{1,0:T(8,128)S(1)} %get-tuple-element.22.perm, bf16[2,2048,128]{2,1,0:T(8,128)(2,1)S(1)} %get-tuple-element.23.u_all, bf16[128,128,256]{2,1,0:T(8,128)(2,1)S(1)} %get-tuple-element.24.v_all, ...), custom_call_target="tpu_custom_call" | custom-call | flops 2147483648 | bytes 16777216 | tf_op jit(solution)/shard_map/products/pallas_call | solution.py:371
  58.7 0.5 collective-permute-start
  59.2 0.0 collective-permute-done.3.refs_10_
  59.3 0.0 collective-permute-done.2.refs_7_
  59.3 0.0 collective-permute-done.1.refs_4_
  59.3 3.9 %collective-permute-done.refs_1_ = bf16[528,128]{1,0:T(8,128)(2,1)S(1)} collective-permute-done((bf16[528,128]{1,0:T(8,128)(2,1)S(1)}, bf16[528,128]{1,0:T(8,128)(2,1)S(1)}, u32[]{:S(2)}, u32[]{:S(2)}) %collective-permute-start) | collective-permute-done | bytes 135200 | tf_op jit(solution)/shard_map/ppermute | solution.py:387
  63.1 1.1 %combine.1 = bf16[2048,128]{1,0:T(8,128)(2,1)} custom-call(f32[512,128]{1,0:T(8,128)S(1)} %get-tuple-element.27.refs_0_, bf16[528,128]{1,0:T(8,128)(2,1)S(1)} %collective-permute-done.refs_1_, f32[4,128]{1,0:T(4,128)S(1)} %get-tuple-element.29.refs_2_, f32[512,128]{1,0:T(8,128)S(1)} %get-tuple-element.30.refs_3_, ...), custom_call_target="tpu_custom_call" | custom-call | tf_op jit(solution)/shard_map/combine/pallas_call | solution.py:388
Async XLA Ops:
  39.3 19.9 %collective-permute-start.3 = (bf16[528,128]{1,0:T(8,128)(2,1)S(1)}, bf16[528,128]{1,0:T(8,128)(2,1)S(1)}, u32[]{:S(2)}, u32[]{:S(2)}) collective-permute-start(bf16[528,128]{1,0:T(8,128)(2,1)S(1)} %get-tuple-element.37), channel_id=1, source_target_pairs={{0,64},{64,0},{1,65},{65,1},{2,66},{66,2},{3,67},{67,3},{4,68},{68... | collective-permute-start | bytes 405512 | tf_op jit(solution)/shard_map/ppermute | solution.py:387
  47.6 11.7 %collective-permute-start.2 = (bf16[528,128]{1,0:T(8,128)(2,1)S(1)}, bf16[528,128]{1,0:T(8,128)(2,1)S(1)}, u32[]{:S(2)}, u32[]{:S(2)}) collective-permute-start(bf16[528,128]{1,0:T(8,128)(2,1)S(1)} %get-tuple-element.34), channel_id=1, source_target_pairs={{0,64},{64,0},{1,65},{65,1},{2,66},{66,2},{3,67},{67,3},{4,68},{68... | collective-permute-start | bytes 405512 | tf_op jit(solution)/shard_map/ppermute | solution.py:387
  52.6 6.6 %collective-permute-start.1 = (bf16[528,128]{1,0:T(8,128)(2,1)S(1)}, bf16[528,128]{1,0:T(8,128)(2,1)S(1)}, u32[]{:S(2)}, u32[]{:S(2)}) collective-permute-start(bf16[528,128]{1,0:T(8,128)(2,1)S(1)} %get-tuple-element.31), channel_id=1, source_target_pairs={{0,64},{64,0},{1,65},{65,1},{2,66},{66,2},{3,67},{67,3},{4,68},{68... | collective-permute-start | bytes 405512 | tf_op jit(solution)/shard_map/ppermute | solution.py:387
  58.7 4.4 %collective-permute-start = (bf16[528,128]{1,0:T(8,128)(2,1)S(1)}, bf16[528,128]{1,0:T(8,128)(2,1)S(1)}, u32[]{:S(2)}, u32[]{:S(2)}) collective-permute-start(bf16[528,128]{1,0:T(8,128)(2,1)S(1)} %get-tuple-element.28), channel_id=1, source_target_pairs={{0,64},{64,0},{1,65},{65,1},{2,66},{66,2},{3,67},{67,3},{4,68},{68... | collective-permute-start | bytes 405512 | tf_op jit(solution)/shard_map/ppermute | solution.py:387

commit v3 on v2

--- a/solution.py
+++ b/solution.py
@@ -15,11 +15,9 @@
 R = 256
 G = 4
 DEEP, AHEAD, BEHIND = 4, 3, 2
-NC = 4
-CB = UB // NC
+CHUNKS = ((0, 7), (7, 13), (13, 16))
 LAG = 6
 SWAPS = 4
-EXTRA = 16
 SLOTS = 640
 
 PLAN = (
@@ -52,15 +50,15 @@
     start = jnp.zeros((UB, 1), jnp.float32)
     marks = jnp.zeros((1, SLOTS), jnp.float32)
     base = jnp.zeros((1, 1), jnp.float32)
-    for c in range(NC):
+    for c, (low, high) in enumerate(CHUNKS):
         marks = marks + jnp.where(lane == c, base, 0.0)
         inside = base
-        for a in range(c * CB, (c + 1) * CB):
+        for a in range(low, high):
             start = start + jnp.where(block == a, inside * G, 0.0)
             inside = inside + steps[a : a + 1, :]
         rounds = jnp.maximum(jnp.floor((inside - base + (DEEP - 1)) * (1.0 / DEEP)), 1.0)
         base = base + rounds * DEEP
-    marks = marks + jnp.where(lane == NC, base, 0.0)
+    marks = marks + jnp.where(lane == len(CHUNKS), base, 0.0)
     place = jnp.sum(jnp.where(owner, rank + start, 0.0), axis=0, keepdims=True)
     match = lax.broadcasted_iota(jnp.int32, (SLOTS, T), 0) == place.astype(jnp.int32)
     number = lax.broadcasted_iota(jnp.int32, (1, T), 1) + 1
@@ -220,8 +218,14 @@
         c.wait_send()
 
 
+def extra(blocks):
+    return -(-3 * blocks // 16) * 16
+
+
 def products_kernel(chunk, perm, u_all, v_all, vt_all, c_all, keep_ref, give_ref, weight_ref, totals, sums):
     f = lax.axis_index("fiber")
+    start_block, end_block = CHUNKS[chunk]
+    blocks = end_block - start_block
     totals[...] = jnp.zeros_like(totals)
     sums[...] = jnp.zeros_like(sums)
     begin = perm[1, chunk]
@@ -251,7 +255,7 @@
                 pltpu.matmul_acc_lhs(scores_acc[r % DEEP][m], u, load_staged_rhs=0)
 
         def finish(s, r):
-            d = rows(s, chunk * CB)
+            d = rows(s, start_block)
             entries = [entry(s, j) for j in range(G)]
             weight_sum = None
             for m in range(2):
@@ -268,7 +272,7 @@
 
         def flush(s, r):
             low, high = prod_acc[r % DEEP]
-            totals[rows(s, chunk * CB), :] += pltpu.matmul_pop(low) + pltpu.matmul_pop(high)
+            totals[rows(s, start_block), :] += pltpu.matmul_pop(low) + pltpu.matmul_pop(high)
 
         def stage(s, r, first=False):
             issue(s + AHEAD, r + AHEAD)
@@ -286,7 +290,11 @@
                 stage(i * DEEP + r, r)
             return carry
 
-        lax.fori_loop(1, rounds, several, 0)
+        def twice(i, carry):
+            return several(2 * i + 2, several(2 * i + 1, carry))
+
+        lax.fori_loop(0, (rounds - 1) // 2, twice, 0)
+        lax.fori_loop((rounds - 1) // 2 * 2 + 1, rounds, several, 0)
         for r in range(BEHIND):
             flush(rounds * DEEP - BEHIND + r, DEEP - BEHIND + r)
         for r in range(AHEAD):
@@ -296,7 +304,7 @@
     pl.run_scoped(scoped, *[pltpu.ACC(n % 2)((TB, R), jnp.float32) for n in range(4 * DEEP)])
 
     sums_row = []
-    for a in range(CB):
+    for a in range(blocks):
         d = pl.ds(a * TB, TB)
         t = totals[d, :]
         low, high = t[:, :TB], t[:, TB:]
@@ -309,22 +317,23 @@
     for _ in range(3):
         parts.append(rest.astype(jnp.bfloat16).astype(jnp.float32))
         rest = rest - parts[-1]
-    parts.append(jnp.zeros((EXTRA - 3 * CB, TB), jnp.float32))
-    give_ref[CB * TB :, :] = jnp.concatenate(parts, axis=0).astype(jnp.bfloat16)
+    parts.append(jnp.zeros((extra(blocks) - 3 * blocks, TB), jnp.float32))
+    give_ref[blocks * TB :, :] = jnp.concatenate(parts, axis=0).astype(jnp.bfloat16)
 
 
 def combine_kernel(*refs):
     out = refs[-1]
-    for c in range(NC):
+    for c, (low, high) in enumerate(CHUNKS):
+        n = high - low
         keep, got, weight = refs[3 * c : 3 * c + 3]
-        sent = got[CB * TB :, :].astype(jnp.float32)
-        total = weight[...] + (sent[:CB] + (sent[CB : 2 * CB] + sent[2 * CB : 3 * CB]))
+        sent = got[n * TB :, :].astype(jnp.float32)
+        total = weight[...] + (sent[:n] + (sent[n : 2 * n] + sent[2 * n : 3 * n]))
         scale = lax.rsqrt(1.0 + total)
-        for a in range(CB):
+        for a in range(n):
             d = pl.ds(a * TB, TB)
             by_row = jnp.broadcast_to(scale[a : a + 1, :], (TB, TB)).T
             row = (keep[d, :] + got[d, :].astype(jnp.float32)) * by_row
-            out[pl.ds((c * CB + a) * TB, TB), :] = row.astype(jnp.bfloat16)
+            out[pl.ds((low + a) * TB, TB), :] = row.astype(jnp.bfloat16)
 
 
 def shards(users, items, tile_users, tile_items, confidence):
@@ -365,20 +374,21 @@
             )
         ]
     )
-    tiles = T // NC
     parts = []
-    for chunk in range(NC):
+    for chunk, (low, high) in enumerate(CHUNKS):
+        n = high - low
+        tiles = T * n // UB
         keep, give, weight = pl.pallas_call(
             functools.partial(products_kernel, chunk),
             name="products",
             in_specs=[smem, vmem, vmem, vmem, vmem],
             out_specs=[vmem, vmem, vmem],
             out_shape=(
-                pltpu.VMEM((CB * TB, TB), f32),
-                pltpu.VMEM((CB * TB + EXTRA, TB), bf16),
-                pltpu.VMEM((CB, TB), f32),
+                pltpu.VMEM((n * TB, TB), f32),
+                pltpu.VMEM((n * TB + extra(n), TB), bf16),
+                pltpu.VMEM((n, TB), f32),
             ),
-            scratch_shapes=[pltpu.VMEM((CB * TB, R), f32), pltpu.VMEM((CB * TB, TB), f32)],
+            scratch_shapes=[pltpu.VMEM((n * TB, R), f32), pltpu.VMEM((n * TB, TB), f32)],
             cost_estimate=pl.CostEstimate(
                 flops=tiles * 4 * TB * TB * R, bytes_accessed=tiles * TB * TB * 8, transcendentals=0
             ),

time: 64.6 us -> 60.7 us (0.940)
  Pallas kernels: 55.9 us -> 52.9 us
    pallas_call x4 -> x3, Pallas kernels: 19.6 us -> 16.7 us  [shards(): pl.pallas_call(functools.partial(products_kernel, chunk), name='products'...]
    ppermute x4 -> x3, starting transfers between devices: 4.45 us -> 3.83 us  [shards(): parts += [keep, lax.ppermute(give, 'fiber', [(0, 1), (1, 0)]), weight]]
    ppermute x4 -> x3, waiting for transfers between devices: 3.87 us -> 3.84 us  [shards(): parts += [keep, lax.ppermute(give, 'fiber', [(0, 1), (1, 0)]), weight]]
  transfers between devices with their start and end apart: 4 -> 3, of which waited for: 1 -> 1; matrix products, arithmetic and copies ran while one was open for 0% -> 0% of each run, Pallas kernels for 24% -> 17%
where the time goes in v3:
time: 60.7 us; the launch traced here: 60.6 us
  Pallas kernels  52.9 us (87%)
  waiting for transfers between devices  3.84 us (6%)
  starting transfers between devices  3.83 us (6%)
    pallas_call x1, Pallas kernels, shards(): pl.pallas_call(gather_kernel, name='gather', in_specs=[hbm] * 5, out_spec...  35.1 us
    pallas_call x3, Pallas kernels, shards(): pl.pallas_call(functools.partial(products_kernel, chunk), name='products'...  16.7 us
    ppermute x3, waiting for transfers between devices, shards(): parts += [keep, lax.ppermute(give, 'fiber', [(0, 1), (1, 0)]), weight]  3.84 us
    ppermute x3, starting transfers between devices, shards(): parts += [keep, lax.ppermute(give, 'fiber', [(0, 1), (1, 0)]), weight]  3.83 us
  transfers between devices with their start and end apart: 3, of which 1 were waited for; matrix products, arithmetic and copies ran while one was open for 0% of the time, Pallas kernels for 17%

profile of v3, /device:TPU:1, one launch (start us, length us, event | category | flops | bytes accessed | tf_op | source)
XLA Modules:
  0.0 60.6 jit_solution(12378432788988338674)
XLA Ops:
  0.0 35.1 %gather.1 = (bf16[2,2048,128]{2,1,0:T(8,128)(2,1)S(1)}, bf16[128,128,256]{2,1,0:T(8,128)(2,1)S(1)}, bf16[128,256,128]{2,1,0:T(8,128)(2,1)S(1)}, bf16[513,128,128]{2,1,0:T(8,128)(2,1)S(1)}, s32[8,640]{1,0:T(8,128)S(1)}) custom-call(bf16[2048,128]{1,0:T(8,128)(2,1)} %users.1, bf16[2,128,256]{2,1,0:T(8,128)(2,1)} %bitcast.5, bf16[512,128,128]{2,1,0:T(8,128)(2,1)} %bitcast.4, ...), custom_call_target="tpu_custom_call" | custom-call | tf_op jit(solution)/shard_map/gather/pallas_call | solution.py:345
  35.1 6.1 %products.4 = (f32[768,128]{1,0:T(8,128)S(1)}, bf16[800,128]{1,0:T(8,128)(2,1)S(1)}, f32[6,128]{1,0:T(8,128)S(1)}) custom-call(s32[8,640]{1,0:T(8,128)S(1)} %get-tuple-element.19.perm, bf16[2,2048,128]{2,1,0:T(8,128)(2,1)S(1)} %get-tuple-element.20.u_all, bf16[128,128,256]{2,1,0:T(8,128)(2,1)S(1)} %get-tuple-element.21.v_all, ...), custom_call_target="tpu_custom_call" | custom-call | flops 3221225472 | bytes 25165824 | tf_op jit(solution)/shard_map/products/pallas_call | solution.py:381
  41.2 1.9 %collective-permute-start.1 = (bf16[800,128]{1,0:T(8,128)(2,1)S(1)}, bf16[800,128]{1,0:T(8,128)(2,1)S(1)}, u32[]{:S(2)}, u32[]{:S(2)}) collective-permute-start(bf16[800,128]{1,0:T(8,128)(2,1)S(1)} %get-tuple-element.28), channel_id=1, source_target_pairs={{0,64},{64,0},{1,65},{65,1},{2,66},{66,2},{3,67},{67,3},{4,68},{68... | collective-permute-start | bytes 614408 | tf_op jit(solution)/shard_map/ppermute | solution.py:397
  43.1 7.0 %products.3 = (f32[896,128]{1,0:T(8,128)S(1)}, bf16[928,128]{1,0:T(8,128)(2,1)S(1)}, f32[7,128]{1,0:T(8,128)S(1)}) custom-call(s32[8,640]{1,0:T(8,128)S(1)} %get-tuple-element.19.perm, bf16[2,2048,128]{2,1,0:T(8,128)(2,1)S(1)} %get-tuple-element.20.u_all, bf16[128,128,256]{2,1,0:T(8,128)(2,1)S(1)} %get-tuple-element.21.v_all, ...), custom_call_target="tpu_custom_call" | custom-call | flops 3758096384 | bytes 29360128 | tf_op jit(solution)/shard_map/products/pallas_call | solution.py:381
  50.1 0.1 collective-permute-start
  50.2 3.6 %products.5 = (f32[384,128]{1,0:T(8,128)S(1)}, bf16[400,128]{1,0:T(8,128)(2,1)S(1)}, f32[3,128]{1,0:T(4,128)S(1)}) custom-call(s32[8,640]{1,0:T(8,128)S(1)} %get-tuple-element.19.perm, bf16[2,2048,128]{2,1,0:T(8,128)(2,1)S(1)} %get-tuple-element.20.u_all, bf16[128,128,256]{2,1,0:T(8,128)(2,1)S(1)} %get-tuple-element.21.v_all, ...), custom_call_target="tpu_custom_call" | custom-call | flops 1610612736 | bytes 12582912 | tf_op jit(solution)/shard_map/products/pallas_call | solution.py:381
  53.8 1.9 %collective-permute-start.2 = (bf16[400,128]{1,0:T(8,128)(2,1)S(1)}, bf16[400,128]{1,0:T(8,128)(2,1)S(1)}, u32[]{:S(2)}, u32[]{:S(2)}) collective-permute-start(bf16[400,128]{1,0:T(8,128)(2,1)S(1)} %get-tuple-element.31), channel_id=1, source_target_pairs={{0,64},{64,0},{1,65},{65,1},{2,66},{66,2},{3,67},{67,3},{4,68},{68... | collective-permute-start | bytes 307208 | tf_op jit(solution)/shard_map/ppermute | solution.py:397
  55.6 3.8 %collective-permute-done.2.refs_7_ = bf16[400,128]{1,0:T(8,128)(2,1)S(1)} collective-permute-done((bf16[400,128]{1,0:T(8,128)(2,1)S(1)}, bf16[400,128]{1,0:T(8,128)(2,1)S(1)}, u32[]{:S(2)}, u32[]{:S(2)}) %collective-permute-start.2) | collective-permute-done | bytes 102432 | tf_op jit(solution)/shard_map/ppermute | solution.py:397
  59.5 0.0 collective-permute-done.1.refs_4_
  59.5 0.0 collective-permute-done.refs_1_
  59.5 1.2 %combine.1 = bf16[2048,128]{1,0:T(8,128)(2,1)} custom-call(f32[896,128]{1,0:T(8,128)S(1)} %get-tuple-element.24.refs_0_, bf16[928,128]{1,0:T(8,128)(2,1)S(1)} %collective-permute-done.refs_1_, f32[7,128]{1,0:T(8,128)S(1)} %get-tuple-element.26.refs_2_, f32[768,128]{1,0:T(8,128)S(1)} %get-tuple-element.27.refs_3_, ...), custom_call_target="tpu_custom_call" | custom-call | tf_op jit(solution)/shard_map/combine/pallas_call | solution.py:398
Async XLA Ops:
  41.2 18.2 %collective-permute-start.1 = (bf16[800,128]{1,0:T(8,128)(2,1)S(1)}, bf16[800,128]{1,0:T(8,128)(2,1)S(1)}, u32[]{:S(2)}, u32[]{:S(2)}) collective-permute-start(bf16[800,128]{1,0:T(8,128)(2,1)S(1)} %get-tuple-element.28), channel_id=1, source_target_pairs={{0,64},{64,0},{1,65},{65,1},{2,66},{66,2},{3,67},{67,3},{4,68},{68... | collective-permute-start | bytes 614408 | tf_op jit(solution)/shard_map/ppermute | solution.py:397
  50.1 9.4 %collective-permute-start = (bf16[928,128]{1,0:T(8,128)(2,1)S(1)}, bf16[928,128]{1,0:T(8,128)(2,1)S(1)}, u32[]{:S(2)}, u32[]{:S(2)}) collective-permute-start(bf16[928,128]{1,0:T(8,128)(2,1)S(1)} %get-tuple-element.25), channel_id=1, source_target_pairs={{0,64},{64,0},{1,65},{65,1},{2,66},{66,2},{3,67},{67,3},{4,68},{68... | collective-permute-start | bytes 712712 | tf_op jit(solution)/shard_map/ppermute | solution.py:397
  53.8 5.7 %collective-permute-start.2 = (bf16[400,128]{1,0:T(8,128)(2,1)S(1)}, bf16[400,128]{1,0:T(8,128)(2,1)S(1)}, u32[]{:S(2)}, u32[]{:S(2)}) collective-permute-start(bf16[400,128]{1,0:T(8,128)(2,1)S(1)} %get-tuple-element.31), channel_id=1, source_target_pairs={{0,64},{64,0},{1,65},{65,1},{2,66},{66,2},{3,67},{67,3},{4,68},{68... | collective-permute-start | bytes 307208 | tf_op jit(solution)/shard_map/ppermute | solution.py:397

commit v4 on v3

--- a/solution.py
+++ b/solution.py
@@ -15,25 +15,25 @@
 R = 256
 G = 4
 DEEP, AHEAD, BEHIND = 4, 3, 2
-CHUNKS = ((0, 7), (7, 13), (13, 16))
+CHUNKS = ((0, 8), (8, 14), (14, 16))
 LAG = 6
 SWAPS = 4
 SLOTS = 640
 
 PLAN = (
-    (0, 0, 0, 1, "M"), (0, 0, -1, 0, "P"), (1, 1, 0, 0, "A"), (0, 0, 0, -1, "P"), (0, 0, 1, 0, "M"),
-    (0, 1, 0, 1, "M"), (0, 1, 0, -1, "P"), (1, 0, 0, 0, "A"), (0, 1, -1, 0, "P"), (0, 1, 1, 0, "M"),
-    (0, 0, -1, 1, "p"), (0, 0, 0, 2, "M"), (1, 1, -1, 0, "A"), (0, 0, 1, 1, "m"), (0, 0, -1, -1, "P"),
-    (0, 0, 2, 0, "P"), (1, 1, 1, 0, "M"), (1, 0, 0, 1, "A"), (1, 1, 0, -1, "P"), (0, 0, 1, -1, "m"),
-    (0, 1, 1, 1, "m"), (1, 0, -1, 0, "P"), (0, 1, -1, 1, "F"), (1, 0, 0, -1, "A"), (0, 1, 1, -1, "m"),
-    (0, 1, 2, 0, "P"), (1, 0, 1, 0, "M"), (0, 0, -1, 2, "P"), (0, 1, 0, 2, "F"), (1, 1, -1, 1, "A"),
-    (0, 0, 1, 2, "M"), (0, 0, 2, -1, "p"), (0, 0, 2, 1, "M"), (1, 1, -1, -1, "p"), (0, 1, -1, -1, "F"),
-    (1, 0, 1, 1, "m"), (1, 0, 2, 0, "P"), (1, 1, 1, 1, "A"), (1, 1, 1, -1, "m"), (1, 0, -1, -1, "P"),
-    (1, 1, 0, 1, "F"), (0, 1, 2, 1, "p"), (0, 1, -1, 2, "M"), (1, 1, 2, 0, "A"), (1, 0, 1, -1, "m"),
-    (0, 0, 2, 2, "p"), (0, 1, 1, 2, "m"), (0, 1, 2, -1, "p"), (1, 0, -1, 1, "A"), (1, 1, -1, 2, "M"),
-    (1, 0, 2, -1, "P"), (1, 1, 2, 1, "m"), (1, 1, 1, 2, "P"), (1, 0, 0, 2, "A"), (1, 1, 2, -1, "m"),
-    (1, 0, -1, 2, "P"), (1, 1, 0, 2, "M"), (1, 0, 1, 2, "P"), (1, 0, 2, 1, "A"), (0, 1, 2, 2, "M"),
-    (1, 0, 2, 2, "P"), (1, 1, 2, 2, "m"),
+    (0, 0, 1, 0, "M"), (0, 0, 0, -1, "P"), (0, 0, 0, 1, "M"), (0, 0, -1, 0, "P"), (1, 0, 0, 0, "A"),
+    (0, 1, -1, 0, "P"), (0, 1, 0, 1, "M"), (0, 1, 0, -1, "P"), (0, 1, 1, 0, "M"), (0, 0, 1, -1, "P"),
+    (0, 0, 1, 1, "M"), (0, 0, -1, -1, "p"), (1, 0, 0, 1, "M"), (1, 1, 1, 0, "A"), (0, 0, 0, 2, "P"),
+    (1, 1, 0, 0, "F"), (1, 0, 1, 0, "M"), (0, 0, -1, 1, "p"), (1, 1, 0, 1, "A"), (0, 1, -1, 1, "M"),
+    (0, 0, 2, 0, "P"), (0, 1, 1, 1, "m"), (1, 0, 0, -1, "P"), (1, 0, -1, 0, "A"), (0, 1, 0, 2, "M"),
+    (0, 1, 2, 0, "P"), (0, 1, 1, -1, "m"), (0, 1, -1, -1, "P"), (0, 0, 2, 1, "m"), (1, 1, 1, -1, "A"),
+    (1, 0, -1, 1, "p"), (1, 0, 0, 2, "M"), (1, 1, 1, 1, "M"), (1, 1, -1, 0, "P"), (1, 1, -1, -1, "A"),
+    (0, 0, 1, 2, "m"), (1, 1, 0, -1, "P"), (0, 0, -1, 2, "M"), (0, 0, 2, -1, "P"), (0, 1, 1, 2, "M"),
+    (1, 0, 1, 1, "A"), (1, 0, -1, -1, "p"), (1, 0, 1, -1, "m"), (0, 1, -1, 2, "p"), (0, 1, 2, -1, "P"),
+    (0, 1, 2, 1, "M"), (1, 0, 2, 0, "A"), (1, 1, 2, -1, "m"), (1, 0, 2, 1, "p"), (1, 0, -1, 2, "M"),
+    (1, 1, 2, 0, "P"), (1, 0, 1, 2, "m"), (1, 1, -1, 2, "P"), (1, 1, 1, 2, "M"), (1, 1, 0, 2, "P"),
+    (1, 1, 2, 1, "m"), (0, 0, 2, 2, "p"), (1, 1, -1, 1, "M"), (1, 0, 2, -1, "p"), (0, 1, 2, 2, "m"),
+    (1, 1, 2, 2, "P"), (1, 0, 2, 2, "M"),
 )
 
 

time: 60.7 us -> 57.3 us (0.944)
  Pallas kernels: 52.9 us -> 50.9 us
  starting transfers between devices: 3.83 us -> 2.48 us
    pallas_call x1, Pallas kernels: 35.1 us -> 33 us  [shards(): pl.pallas_call(gather_kernel, name='gather', in_specs=[hbm] * 5, out_spec...]
    ppermute x3, starting transfers between devices: 3.83 us -> 2.48 us  [shards(): parts += [keep, lax.ppermute(give, 'fiber', [(0, 1), (1, 0)]), weight]]
  transfers between devices with their start and end apart: 3 -> 3, of which waited for: 1 -> 1; matrix products, arithmetic and copies ran while one was open for 0% -> 0% of each run, Pallas kernels for 17% -> 16%
where the time goes in v4:
time: 57.3 us; the launch traced here: 57.2 us
  Pallas kernels  50.9 us (89%)
  waiting for transfers between devices  3.74 us (7%)
  starting transfers between devices  2.48 us (4%)
    pallas_call x1, Pallas kernels, shards(): pl.pallas_call(gather_kernel, name='gather', in_specs=[hbm] * 5, out_spec...  33 us
    pallas_call x3, Pallas kernels, shards(): pl.pallas_call(functools.partial(products_kernel, chunk), name='products'...  16.7 us
    ppermute x3, waiting for transfers between devices, shards(): parts += [keep, lax.ppermute(give, 'fiber', [(0, 1), (1, 0)]), weight]  3.74 us
    ppermute x3, starting transfers between devices, shards(): parts += [keep, lax.ppermute(give, 'fiber', [(0, 1), (1, 0)]), weight]  2.48 us
    pallas_call x1, Pallas kernels, shards(): pl.pallas_call(combine_kernel, name='combine', in_specs=[vmem] * len(part...  1.15 us
  transfers between devices with their start and end apart: 3, of which 1 were waited for; matrix products, arithmetic and copies ran while one was open for 0% of the time, Pallas kernels for 16%

profile of v4, /device:TPU:1, one launch (start us, length us, event | category | flops | bytes accessed | tf_op | source)
XLA Modules:
  0.0 57.2 jit_solution(11447491880018122213)
XLA Ops:
  0.0 33.0 %gather.1 = (bf16[2,2048,128]{2,1,0:T(8,128)(2,1)S(1)}, bf16[128,128,256]{2,1,0:T(8,128)(2,1)S(1)}, bf16[128,256,128]{2,1,0:T(8,128)(2,1)S(1)}, bf16[513,128,128]{2,1,0:T(8,128)(2,1)S(1)}, s32[8,640]{1,0:T(8,128)S(1)}) custom-call(bf16[2048,128]{1,0:T(8,128)(2,1)} %users.1, bf16[2,128,256]{2,1,0:T(8,128)(2,1)} %bitcast.5, bf16[512,128,128]{2,1,0:T(8,128)(2,1)} %bitcast.4, ...), custom_call_target="tpu_custom_call" | custom-call | tf_op jit(solution)/shard_map/gather/pallas_call | solution.py:345
  33.0 7.8 %products.3 = (f32[1024,128]{1,0:T(8,128)S(1)}, bf16[1056,128]{1,0:T(8,128)(2,1)S(1)}, f32[8,128]{1,0:T(8,128)S(1)}) custom-call(s32[8,640]{1,0:T(8,128)S(1)} %get-tuple-element.19.perm, bf16[2,2048,128]{2,1,0:T(8,128)(2,1)S(1)} %get-tuple-element.20.u_all, bf16[128,128,256]{2,1,0:T(8,128)(2,1)S(1)} %get-tuple-element.21.v_all, ...), custom_call_target="tpu_custom_call" | custom-call | flops 4294967296 | bytes 33554432 | tf_op jit(solution)/shard_map/products/pallas_call | solution.py:381
  40.8 0.3 collective-permute-start
  41.1 5.8 %products.4 = (f32[768,128]{1,0:T(8,128)S(1)}, bf16[800,128]{1,0:T(8,128)(2,1)S(1)}, f32[6,128]{1,0:T(8,128)S(1)}) custom-call(s32[8,640]{1,0:T(8,128)S(1)} %get-tuple-element.19.perm, bf16[2,2048,128]{2,1,0:T(8,128)(2,1)S(1)} %get-tuple-element.20.u_all, bf16[128,128,256]{2,1,0:T(8,128)(2,1)S(1)} %get-tuple-element.21.v_all, ...), custom_call_target="tpu_custom_call" | custom-call | flops 3221225472 | bytes 25165824 | tf_op jit(solution)/shard_map/products/pallas_call | solution.py:381
  46.9 2.1 %collective-permute-start.1 = (bf16[800,128]{1,0:T(8,128)(2,1)S(1)}, bf16[800,128]{1,0:T(8,128)(2,1)S(1)}, u32[]{:S(2)}, u32[]{:S(2)}) collective-permute-start(bf16[800,128]{1,0:T(8,128)(2,1)S(1)} %get-tuple-element.28), channel_id=1, source_target_pairs={{0,64},{64,0},{1,65},{65,1},{2,66},{66,2},{3,67},{67,3},{4,68},{68... | collective-permute-start | bytes 614408 | tf_op jit(solution)/shard_map/ppermute | solution.py:397
  49.1 3.1 %products.5 = (f32[256,128]{1,0:T(8,128)S(1)}, bf16[272,128]{1,0:T(8,128)(2,1)S(1)}, f32[2,128]{1,0:T(2,128)S(1)}) custom-call(s32[8,640]{1,0:T(8,128)S(1)} %get-tuple-element.19.perm, bf16[2,2048,128]{2,1,0:T(8,128)(2,1)S(1)} %get-tuple-element.20.u_all, bf16[128,128,256]{2,1,0:T(8,128)(2,1)S(1)} %get-tuple-element.21.v_all, ...), custom_call_target="tpu_custom_call" | custom-call | flops 1073741824 | bytes 8388608 | tf_op jit(solution)/shard_map/products/pallas_call | solution.py:381
  52.2 0.1 collective-permute-start.2
  52.3 3.7 %collective-permute-done.2.refs_7_ = bf16[272,128]{1,0:T(8,128)(2,1)S(1)} collective-permute-done((bf16[272,128]{1,0:T(8,128)(2,1)S(1)}, bf16[272,128]{1,0:T(8,128)(2,1)S(1)}, u32[]{:S(2)}, u32[]{:S(2)}) %collective-permute-start.2) | collective-permute-done | bytes 69664 | tf_op jit(solution)/shard_map/ppermute | solution.py:397
  56.0 0.0 collective-permute-done.1.refs_4_
  56.0 0.0 collective-permute-done.refs_1_
  56.0 1.1 %combine.1 = bf16[2048,128]{1,0:T(8,128)(2,1)} custom-call(f32[1024,128]{1,0:T(8,128)S(1)} %get-tuple-element.24.refs_0_, bf16[1056,128]{1,0:T(8,128)(2,1)S(1)} %collective-permute-done.refs_1_, f32[8,128]{1,0:T(8,128)S(1)} %get-tuple-element.26.refs_2_, f32[768,128]{1,0:T(8,128)S(1)} %get-tuple-element.27.refs_3_, ...), custom_call_target="tpu_custom_call" | custom-call | tf_op jit(solution)/shard_map/combine/pallas_call | solution.py:398
Async XLA Ops:
  40.8 15.2 %collective-permute-start = (bf16[1056,128]{1,0:T(8,128)(2,1)S(1)}, bf16[1056,128]{1,0:T(8,128)(2,1)S(1)}, u32[]{:S(2)}, u32[]{:S(2)}) collective-permute-start(bf16[1056,128]{1,0:T(8,128)(2,1)S(1)} %get-tuple-element.25), channel_id=1, source_target_pairs={{0,64},{64,0},{1,65},{65,1},{2,66},{66,2},{3,67},{67,3},{4,68},{68... | collective-permute-start | bytes 811016 | tf_op jit(solution)/shard_map/ppermute | solution.py:397
  46.9 9.1 %collective-permute-start.1 = (bf16[800,128]{1,0:T(8,128)(2,1)S(1)}, bf16[800,128]{1,0:T(8,128)(2,1)S(1)}, u32[]{:S(2)}, u32[]{:S(2)}) collective-permute-start(bf16[800,128]{1,0:T(8,128)(2,1)S(1)} %get-tuple-element.28), channel_id=1, source_target_pairs={{0,64},{64,0},{1,65},{65,1},{2,66},{66,2},{3,67},{67,3},{4,68},{68... | collective-permute-start | bytes 614408 | tf_op jit(solution)/shard_map/ppermute | solution.py:397
  52.2 3.8 %collective-permute-start.2 = (bf16[272,128]{1,0:T(8,128)(2,1)S(1)}, bf16[272,128]{1,0:T(8,128)(2,1)S(1)}, u32[]{:S(2)}, u32[]{:S(2)}) collective-permute-start(bf16[272,128]{1,0:T(8,128)(2,1)S(1)} %get-tuple-element.31), channel_id=1, source_target_pairs={{0,64},{64,0},{1,65},{65,1},{2,66},{66,2},{3,67},{67,3},{4,68},{68... | collective-permute-start | bytes 208904 | tf_op jit(solution)/shard_map/ppermute | solution.py:397

commit v5 on v4

--- a/solution.py
+++ b/solution.py
@@ -15,25 +15,25 @@
 R = 256
 G = 4
 DEEP, AHEAD, BEHIND = 4, 3, 2
-CHUNKS = ((0, 8), (8, 14), (14, 16))
+CHUNKS = ((0, 8), (8, 13), (13, 16))
 LAG = 6
 SWAPS = 4
 SLOTS = 640
 
 PLAN = (
-    (0, 0, 1, 0, "M"), (0, 0, 0, -1, "P"), (0, 0, 0, 1, "M"), (0, 0, -1, 0, "P"), (1, 0, 0, 0, "A"),
-    (0, 1, -1, 0, "P"), (0, 1, 0, 1, "M"), (0, 1, 0, -1, "P"), (0, 1, 1, 0, "M"), (0, 0, 1, -1, "P"),
-    (0, 0, 1, 1, "M"), (0, 0, -1, -1, "p"), (1, 0, 0, 1, "M"), (1, 1, 1, 0, "A"), (0, 0, 0, 2, "P"),
-    (1, 1, 0, 0, "F"), (1, 0, 1, 0, "M"), (0, 0, -1, 1, "p"), (1, 1, 0, 1, "A"), (0, 1, -1, 1, "M"),
-    (0, 0, 2, 0, "P"), (0, 1, 1, 1, "m"), (1, 0, 0, -1, "P"), (1, 0, -1, 0, "A"), (0, 1, 0, 2, "M"),
-    (0, 1, 2, 0, "P"), (0, 1, 1, -1, "m"), (0, 1, -1, -1, "P"), (0, 0, 2, 1, "m"), (1, 1, 1, -1, "A"),
-    (1, 0, -1, 1, "p"), (1, 0, 0, 2, "M"), (1, 1, 1, 1, "M"), (1, 1, -1, 0, "P"), (1, 1, -1, -1, "A"),
-    (0, 0, 1, 2, "m"), (1, 1, 0, -1, "P"), (0, 0, -1, 2, "M"), (0, 0, 2, -1, "P"), (0, 1, 1, 2, "M"),
-    (1, 0, 1, 1, "A"), (1, 0, -1, -1, "p"), (1, 0, 1, -1, "m"), (0, 1, -1, 2, "p"), (0, 1, 2, -1, "P"),
-    (0, 1, 2, 1, "M"), (1, 0, 2, 0, "A"), (1, 1, 2, -1, "m"), (1, 0, 2, 1, "p"), (1, 0, -1, 2, "M"),
-    (1, 1, 2, 0, "P"), (1, 0, 1, 2, "m"), (1, 1, -1, 2, "P"), (1, 1, 1, 2, "M"), (1, 1, 0, 2, "P"),
-    (1, 1, 2, 1, "m"), (0, 0, 2, 2, "p"), (1, 1, -1, 1, "M"), (1, 0, 2, -1, "p"), (0, 1, 2, 2, "m"),
-    (1, 1, 2, 2, "P"), (1, 0, 2, 2, "M"),
+    (0, 0, 1, 0, "M"), (0, 0, -1, 0, "P"), (0, 0, 0, -1, "P"), (0, 0, 0, 1, "M"), (1, 0, 0, 0, "A"),
+    (0, 1, 0, 1, "M"), (0, 1, -1, 0, "P"), (0, 1, 0, -1, "P"), (0, 1, 1, 0, "M"), (0, 0, 1, -1, "P"),
+    (0, 0, 1, 1, "M"), (0, 0, 2, 0, "P"), (1, 0, 0, 1, "M"), (1, 1, 1, 0, "A"), (0, 0, -1, -1, "P"),
+    (1, 0, 1, 0, "M"), (1, 1, 0, 0, "F"), (0, 0, 0, 2, "P"), (0, 1, 1, 1, "m"), (1, 1, -1, 0, "A"),
+    (0, 0, -1, 1, "p"), (0, 1, 0, 2, "M"), (1, 1, 0, -1, "A"), (1, 0, 0, -1, "P"), (0, 1, -1, 1, "M"),
+    (1, 0, -1, 0, "P"), (0, 0, 2, -1, "m"), (0, 1, 2, 0, "P"), (0, 1, 1, -1, "F"), (1, 1, 1, -1, "A"),
+    (1, 0, 0, 2, "M"), (0, 1, -1, -1, "p"), (1, 1, 1, 1, "M"), (0, 0, 1, 2, "P"), (1, 1, 2, 0, "A"),
+    (1, 1, 0, 1, "F"), (1, 0, 2, 0, "M"), (1, 0, -1, 1, "p"), (0, 1, 1, 2, "M"), (0, 0, 2, 1, "p"),
+    (1, 0, 1, 1, "A"), (1, 1, -1, 1, "M"), (1, 1, 0, 2, "P"), (0, 0, -1, 2, "M"), (1, 1, -1, -1, "p"),
+    (1, 1, 2, -1, "A"), (1, 0, 1, 2, "m"), (0, 1, 2, 1, "p"), (1, 1, 1, 2, "M"), (0, 1, 2, -1, "P"),
+    (1, 0, 1, -1, "A"), (0, 0, 2, 2, "m"), (0, 1, -1, 2, "P"), (1, 0, -1, 2, "M"), (1, 0, 2, -1, "P"),
+    (1, 0, -1, -1, "A"), (0, 1, 2, 2, "m"), (1, 0, 2, 1, "p"), (1, 1, -1, 2, "M"), (1, 1, 2, 1, "p"),
+    (1, 0, 2, 2, "m"), (1, 1, 2, 2, "P"),
 )
 
 
@@ -321,9 +321,10 @@
     give_ref[blocks * TB :, :] = jnp.concatenate(parts, axis=0).astype(jnp.bfloat16)
 
 
-def combine_kernel(*refs):
-    out = refs[-1]
-    for c, (low, high) in enumerate(CHUNKS):
+def combine_kernel(chunks, *refs):
+    out, made, done = refs[-3:]
+    base = chunks[0][0] * TB
+    for c, (low, high) in enumerate(chunks):
         n = high - low
         keep, got, weight = refs[3 * c : 3 * c + 3]
         sent = got[n * TB :, :].astype(jnp.float32)
@@ -333,7 +334,10 @@
             d = pl.ds(a * TB, TB)
             by_row = jnp.broadcast_to(scale[a : a + 1, :], (TB, TB)).T
             row = (keep[d, :] + got[d, :].astype(jnp.float32)) * by_row
-            out[pl.ds((low + a) * TB, TB), :] = row.astype(jnp.bfloat16)
+            made[pl.ds((low + a) * TB - base, TB), :] = row.astype(jnp.bfloat16)
+    copy = pltpu.make_async_copy(made, out.at[pl.ds(base, made.shape[0])], done)
+    copy.start()
+    copy.wait()
 
 
 def shards(users, items, tile_users, tile_items, confidence):
@@ -395,14 +399,23 @@
             compiler_params=pltpu.CompilerParams(vmem_limit_bytes=8 << 20),
         )(perm, u_all, v_all, vt_all, c_all)
         parts += [keep, lax.ppermute(give, "fiber", [(0, 1), (1, 0)]), weight]
-    return pl.pallas_call(
-        combine_kernel,
-        name="combine",
-        in_specs=[vmem] * len(parts),
-        out_specs=vmem,
-        out_shape=jax.ShapeDtypeStruct((rows, TB), bf16),
-        compiler_params=pltpu.CompilerParams(vmem_limit_bytes=8 << 20),
-    )(*parts)
+    out = None
+    for chunks in (CHUNKS[:-1], CHUNKS[-1:]):
+        own, parts = parts[: 3 * len(chunks)], parts[3 * len(chunks) :]
+        count = chunks[-1][1] - chunks[0][0]
+        before = [] if out is None else [out]
+        out = pl.pallas_call(
+            functools.partial(combine_kernel, chunks),
+            name="combine",
+            in_specs=[vmem] * len(own) + [hbm] * len(before),
+            out_specs=hbm,
+            out_shape=jax.ShapeDtypeStruct((rows, TB), bf16),
+            input_output_aliases={len(own): 0} if before else {},
+            scratch_shapes=[pltpu.VMEM((count * TB, TB), bf16), pltpu.SemaphoreType.DMA],
+            cost_estimate=pl.CostEstimate(flops=count * TB * TB * 4, bytes_accessed=count * TB * TB * 10, transcendentals=0),
+            compiler_params=pltpu.CompilerParams(vmem_limit_bytes=8 << 20),
+        )(*own, *before)
+    return out
 
 
 def solution(mesh):

time: 57.3 us -> 56.4 us (0.984)
  waiting for transfers between devices: 3.74 us -> 2.05 us
  Pallas kernels: 50.9 us -> 51.9 us
    ppermute x3, waiting for transfers between devices: 3.74 us -> 2.05 us  [shards(): parts += [keep, lax.ppermute(give, 'fiber', [(0, 1), (1, 0)]), weight]]
    pallas_call x1 -> x2, Pallas kernels: 1.15 us -> 1.89 us  [shards(): pl.pallas_call(functools.partial(combine_kernel, chunks), name='combine',...]
  transfers between devices with their start and end apart: 3 -> 3, of which waited for: 1 -> 1; matrix products, arithmetic and copies ran while one was open for 0% -> 0% of each run, Pallas kernels for 16% -> 19%
where the time goes in v5:
time: 56.4 us
  Pallas kernels  51.9 us (92%)
  starting transfers between devices  2.52 us (4%)
  waiting for transfers between devices  2.05 us (4%)
    pallas_call x1, Pallas kernels, shards(): pl.pallas_call(gather_kernel, name='gather', in_specs=[hbm] * 5, out_spec...  32.8 us
    pallas_call x3, Pallas kernels, shards(): pl.pallas_call(functools.partial(products_kernel, chunk), name='products'...  17.2 us
    ppermute x3, starting transfers between devices, shards(): parts += [keep, lax.ppermute(give, 'fiber', [(0, 1), (1, 0)]), weight]  2.52 us
    ppermute x3, waiting for transfers between devices, shards(): parts += [keep, lax.ppermute(give, 'fiber', [(0, 1), (1, 0)]), weight]  2.05 us
    pallas_call x2, Pallas kernels, shards(): pl.pallas_call(functools.partial(combine_kernel, chunks), name='combine',...  1.89 us
  transfers between devices with their start and end apart: 3, of which 1 were waited for; matrix products, arithmetic and copies ran while one was open for 0% of the time, Pallas kernels for 19%

profile of v5, /device:TPU:1, one launch (start us, length us, event | category | flops | bytes accessed | tf_op | source)
XLA Modules:
  0.0 56.4 jit_solution(1140574164179655342)
XLA Ops:
  0.0 32.8 %gather.1 = (bf16[2,2048,128]{2,1,0:T(8,128)(2,1)S(1)}, bf16[128,128,256]{2,1,0:T(8,128)(2,1)S(1)}, bf16[128,256,128]{2,1,0:T(8,128)(2,1)S(1)}, bf16[513,128,128]{2,1,0:T(8,128)(2,1)S(1)}, s32[8,640]{1,0:T(8,128)S(1)}) custom-call(bf16[2048,128]{1,0:T(8,128)(2,1)} %users.1, bf16[2,128,256]{2,1,0:T(8,128)(2,1)} %bitcast.5, bf16[512,128,128]{2,1,0:T(8,128)(2,1)} %bitcast.4, ...), custom_call_target="tpu_custom_call" | custom-call | tf_op jit(solution)/shard_map/gather/pallas_call | solution.py:349
  32.8 7.8 %products.4 = (f32[1024,128]{1,0:T(8,128)S(1)}, bf16[1056,128]{1,0:T(8,128)(2,1)S(1)}, f32[8,128]{1,0:T(8,128)S(1)}) custom-call(s32[8,640]{1,0:T(8,128)S(1)} %get-tuple-element.19.perm, bf16[2,2048,128]{2,1,0:T(8,128)(2,1)S(1)} %get-tuple-element.20.u_all, bf16[128,128,256]{2,1,0:T(8,128)(2,1)S(1)} %get-tuple-element.21.v_all, ...), custom_call_target="tpu_custom_call" | custom-call | flops 4294967296 | bytes 33554432 | tf_op jit(solution)/shard_map/products/pallas_call | solution.py:385
  40.6 0.9 %collective-permute-start.1 = (bf16[1056,128]{1,0:T(8,128)(2,1)S(1)}, bf16[1056,128]{1,0:T(8,128)(2,1)S(1)}, u32[]{:S(2)}, u32[]{:S(2)}) collective-permute-start(bf16[1056,128]{1,0:T(8,128)(2,1)S(1)} %get-tuple-element.28), channel_id=1, source_target_pairs={{0,64},{64,0},{1,65},{65,1},{2,66},{66,2},{3,67},{67,3},{4,68},{68... | collective-permute-start | bytes 811016 | tf_op jit(solution)/shard_map/ppermute | solution.py:401
  41.5 5.5 %products.5 = (f32[640,128]{1,0:T(8,128)S(1)}, bf16[656,128]{1,0:T(8,128)(2,1)S(1)}, f32[5,128]{1,0:T(8,128)S(1)}) custom-call(s32[8,640]{1,0:T(8,128)S(1)} %get-tuple-element.19.perm, bf16[2,2048,128]{2,1,0:T(8,128)(2,1)S(1)} %get-tuple-element.20.u_all, bf16[128,128,256]{2,1,0:T(8,128)(2,1)S(1)} %get-tuple-element.21.v_all, ...), custom_call_target="tpu_custom_call" | custom-call | flops 2684354560 | bytes 20971520 | tf_op jit(solution)/shard_map/products/pallas_call | solution.py:385
  47.0 0.7 %collective-permute-start.2 = (bf16[656,128]{1,0:T(8,128)(2,1)S(1)}, bf16[656,128]{1,0:T(8,128)(2,1)S(1)}, u32[]{:S(2)}, u32[]{:S(2)}) collective-permute-start(bf16[656,128]{1,0:T(8,128)(2,1)S(1)} %get-tuple-element.31), channel_id=1, source_target_pairs={{0,64},{64,0},{1,65},{65,1},{2,66},{66,2},{3,67},{67,3},{4,68},{68... | collective-permute-start | bytes 503816 | tf_op jit(solution)/shard_map/ppermute | solution.py:401
  47.7 3.9 %products.3 = (f32[384,128]{1,0:T(8,128)S(1)}, bf16[400,128]{1,0:T(8,128)(2,1)S(1)}, f32[3,128]{1,0:T(4,128)S(1)}) custom-call(s32[8,640]{1,0:T(8,128)S(1)} %get-tuple-element.19.perm, bf16[2,2048,128]{2,1,0:T(8,128)(2,1)S(1)} %get-tuple-element.20.u_all, bf16[128,128,256]{2,1,0:T(8,128)(2,1)S(1)} %get-tuple-element.21.v_all, ...), custom_call_target="tpu_custom_call" | custom-call | flops 1610612736 | bytes 12582912 | tf_op jit(solution)/shard_map/products/pallas_call | solution.py:385
  51.6 0.9 %collective-permute-start = (bf16[400,128]{1,0:T(8,128)(2,1)S(1)}, bf16[400,128]{1,0:T(8,128)(2,1)S(1)}, u32[]{:S(2)}, u32[]{:S(2)}) collective-permute-start(bf16[400,128]{1,0:T(8,128)(2,1)S(1)} %get-tuple-element.25), channel_id=1, source_target_pairs={{0,64},{64,0},{1,65},{65,1},{2,66},{66,2},{3,67},{67,3},{4,68},{68... | collective-permute-start | bytes 307208 | tf_op jit(solution)/shard_map/ppermute | solution.py:401
  52.5 0.0 collective-permute-done.2.refs_4_
  52.5 0.0 collective-permute-done.1.refs_1_
  52.5 1.1 %combine.2.refs_3_ = bf16[2048,128]{1,0:T(8,128)(2,1)} custom-call(f32[1024,128]{1,0:T(8,128)S(1)} %get-tuple-element.27.refs_0_, bf16[1056,128]{1,0:T(8,128)(2,1)S(1)} %collective-permute-done.1.refs_1_, f32[8,128]{1,0:T(8,128)S(1)} %get-tuple-element.29.refs_2_, f32[640,128]{1,0:T(8,128)S(1)} %get-tuple-element.30.refs_3_, ...), custom_call_target="tpu_custom_call" | custom-call | flops 851968 | bytes 2129920 | tf_op jit(solution)/shard_map/combine/pallas_call | solution.py:407
  53.6 2.0 %collective-permute-done.refs_1_ = bf16[400,128]{1,0:T(8,128)(2,1)S(1)} collective-permute-done((bf16[400,128]{1,0:T(8,128)(2,1)S(1)}, bf16[400,128]{1,0:T(8,128)(2,1)S(1)}, u32[]{:S(2)}, u32[]{:S(2)}) %collective-permute-start) | collective-permute-done | bytes 102432 | tf_op jit(solution)/shard_map/ppermute | solution.py:401
  55.6 0.8 %combine.3 = bf16[2048,128]{1,0:T(8,128)(2,1)} custom-call(f32[384,128]{1,0:T(8,128)S(1)} %get-tuple-element.24.refs_0_, bf16[400,128]{1,0:T(8,128)(2,1)S(1)} %collective-permute-done.refs_1_, f32[3,128]{1,0:T(4,128)S(1)} %get-tuple-element.26.refs_2_, bf16[2048,128]{1,0:T(8,128)(2,1)} %combine.2.refs_3_), custom_call_target="tpu_custom_call", output_to_operand_aliasing={{}: (3, {})} | custom-call | flops 196608 | bytes 491520 | tf_op jit(solution)/shard_map/combine/pallas_call | solution.py:407
Async XLA Ops:
  40.6 11.9 %collective-permute-start.1 = (bf16[1056,128]{1,0:T(8,128)(2,1)S(1)}, bf16[1056,128]{1,0:T(8,128)(2,1)S(1)}, u32[]{:S(2)}, u32[]{:S(2)}) collective-permute-start(bf16[1056,128]{1,0:T(8,128)(2,1)S(1)} %get-tuple-element.28), channel_id=1, source_target_pairs={{0,64},{64,0},{1,65},{65,1},{2,66},{66,2},{3,67},{67,3},{4,68},{68... | collective-permute-start | bytes 811016 | tf_op jit(solution)/shard_map/ppermute | solution.py:401
  47.0 5.5 %collective-permute-start.2 = (bf16[656,128]{1,0:T(8,128)(2,1)S(1)}, bf16[656,128]{1,0:T(8,128)(2,1)S(1)}, u32[]{:S(2)}, u32[]{:S(2)}) collective-permute-start(bf16[656,128]{1,0:T(8,128)(2,1)S(1)} %get-tuple-element.31), channel_id=1, source_target_pairs={{0,64},{64,0},{1,65},{65,1},{2,66},{66,2},{3,67},{67,3},{4,68},{68... | collective-permute-start | bytes 503816 | tf_op jit(solution)/shard_map/ppermute | solution.py:401
  51.6 4.1 %collective-permute-start = (bf16[400,128]{1,0:T(8,128)(2,1)S(1)}, bf16[400,128]{1,0:T(8,128)(2,1)S(1)}, u32[]{:S(2)}, u32[]{:S(2)}) collective-permute-start(bf16[400,128]{1,0:T(8,128)(2,1)S(1)} %get-tuple-element.25), channel_id=1, source_target_pairs={{0,64},{64,0},{1,65},{65,1},{2,66},{66,2},{3,67},{67,3},{4,68},{68... | collective-permute-start | bytes 307208 | tf_op jit(solution)/shard_map/ppermute | solution.py:401
